TPU v7x, 32 devices: a whole 2x2x4 slice. The times are simulated.
32 devices in a mesh: wide: 8 (over z, x), narrow: 4 (over y, core).
Axes of the slice: x: 2, y: 2, z: 4, core: 2. Of those that a mesh axis runs over, the one named last changes fastest.
Arguments:
- displacement: float32 [3, 3, 128, 128, 384], P(None, None, 'wide', 'narrow'), may hold values from -6 to 6
- material: int32 [128, 128, 24], P('wide', 'narrow'), may hold values 0 or 1
- level_set: float32 [384, 128, 128], P('wide', 'narrow'), may hold values from -6 to 6
Outputs:
- level_next: float32 [384, 128, 128], P('wide', 'narrow')
- speed: float32 [384, 128, 128], P('wide', 'narrow')
All inputs are finite; a program needn't handle non-finite values. No bound on the sum of `material` on one device may be relied on, other than what follows from the above.
Results may differ from a plain program's by a relative error of at most 0.00002.
Values sent between devices are 32-bit elements; how exact they have to be, the bound alone decides.
A program may use at most 192 MiB of HBM per device.

v0:
```python
import jax
import jax.numpy as jnp
from jax import lax
from jax.sharding import PartitionSpec as P

BZ = 16
EXT_PASSES = 4
HJ_STEPS = 3


SHEAR = 0.384615
LAME = 0.576923
WENO_EPS = 1e-06
TIME_STEP = 0.3
VAL_TAPS = (1.0 / 48.0, 23.0 / 48.0, 23.0 / 48.0, 1.0 / 48.0)
DER_TAPS = (-1.0 / 8.0, -5.0 / 8.0, 5.0 / 8.0, 1.0 / 8.0)


def with_halo(block, sides, width):
    for axis, dim in sides:
        count = lax.axis_size(axis)
        forward = [(i, i + 1) for i in range(count - 1)]
        backward = [(target, source) for source, target in forward]
        low = lax.ppermute(
            lax.slice_in_dim(block, block.shape[dim] - width, None, axis=dim), axis, forward
        )
        high = lax.ppermute(lax.slice_in_dim(block, 0, width, axis=dim), axis, backward)
        block = jnp.concatenate([low, block, high], axis=dim)
    return block


def apply_taps(padded, taps, axis, count):
    total = taps[0] * lax.slice_in_dim(padded, 1, 1 + count, axis=axis)
    for k in range(1, 4):
        total = total + taps[k] * lax.slice_in_dim(padded, 1 + k, 1 + k + count, axis=axis)
    return total


def strain_energy(grad_x, grad_y, grad_z, stiffness):
    exx = grad_x[:, 0]
    eyy = grad_y[:, 1]
    ezz = grad_z[:, 2]
    exy = 0.5 * (grad_y[:, 0] + grad_x[:, 1])
    exz = 0.5 * (grad_z[:, 0] + grad_x[:, 2])
    eyz = 0.5 * (grad_z[:, 1] + grad_y[:, 2])
    trace = exx + eyy + ezz
    square = exx * exx + eyy * eyy + ezz * ezz + 2.0 * (exy * exy + exz * exz + eyz * eyz)
    density = SHEAR * square + 0.5 * LAME * trace * trace
    return stiffness * jnp.sum(density, axis=0)


def neighbour_mean(padded):
    wider = jnp.pad(padded, ((0, 0), (0, 0), (1, 1)))
    total = wider[2:, 1:-1, 1:-1] + wider[:-2, 1:-1, 1:-1]
    total = total + wider[1:-1, 2:, 1:-1] + wider[1:-1, :-2, 1:-1]
    total = total + wider[1:-1, 1:-1, 2:] + wider[1:-1, 1:-1, :-2]
    return total * (1.0 / 6.0)


def weno_side(v1, v2, v3, v4, v5):
    p_one = v1 / 3.0 - 7.0 * v2 / 6.0 + 11.0 * v3 / 6.0
    p_two = -v2 / 6.0 + 5.0 * v3 / 6.0 + v4 / 3.0
    p_three = v3 / 3.0 + 5.0 * v4 / 6.0 - v5 / 6.0
    b_one = 13.0 / 12.0 * (v1 - 2.0 * v2 + v3) ** 2 + 0.25 * (v1 - 4.0 * v2 + 3.0 * v3) ** 2
    b_two = 13.0 / 12.0 * (v2 - 2.0 * v3 + v4) ** 2 + 0.25 * (v2 - v4) ** 2
    b_three = 13.0 / 12.0 * (v3 - 2.0 * v4 + v5) ** 2 + 0.25 * (3.0 * v3 - 4.0 * v4 + v5) ** 2
    a_one = 0.1 / (WENO_EPS + b_one) ** 2
    a_two = 0.6 / (WENO_EPS + b_two) ** 2
    a_three = 0.3 / (WENO_EPS + b_three) ** 2
    return (a_one * p_one + a_two * p_two + a_three * p_three) / (a_one + a_two + a_three)


def march_step(padded, speed):
    wider = jnp.pad(padded, ((0, 0), (0, 0), (3, 3)), constant_values=1.0)
    size_z = padded.shape[0] - 6
    size_y = padded.shape[1] - 6
    size_x = padded.shape[2]
    centre = wider[3 : 3 + size_z, 3 : 3 + size_y, 3 : 3 + size_x]
    lines = (
        wider[:, 3 : 3 + size_y, 3 : 3 + size_x],
        wider[3 : 3 + size_z, :, 3 : 3 + size_x],
        wider[3 : 3 + size_z, 3 : 3 + size_y, :],
    )
    grow_plus = None
    grow_minus = None
    for axis in range(3):
        line = lines[axis]
        count = centre.shape[axis]
        diffs = lax.slice_in_dim(line, 1, count + 6, axis=axis) - lax.slice_in_dim(
            line, 0, count + 5, axis=axis
        )
        parts = [lax.slice_in_dim(diffs, k, k + count, axis=axis) for k in range(6)]
        minus = weno_side(parts[0], parts[1], parts[2], parts[3], parts[4])
        plus = weno_side(parts[5], parts[4], parts[3], parts[2], parts[1])
        term_p = jnp.maximum(jnp.maximum(minus, 0.0) ** 2, jnp.minimum(plus, 0.0) ** 2)
        term_m = jnp.maximum(jnp.minimum(minus, 0.0) ** 2, jnp.maximum(plus, 0.0) ** 2)
        grow_plus = term_p if grow_plus is None else grow_plus + term_p
        grow_minus = term_m if grow_minus is None else grow_minus + term_m
    return centre - TIME_STEP * (
        jnp.maximum(speed, 0.0) * jnp.sqrt(grow_plus)
        + jnp.minimum(speed, 0.0) * jnp.sqrt(grow_minus)
    )


def inner_region(array, margin):
    return array[margin : array.shape[0] - margin, margin : array.shape[1] - margin]


def ghost_fill(array, margin, value):
    own_z = array.shape[0] - 2 * margin
    own_y = array.shape[1] - 2 * margin
    pos_z = lax.axis_index("wide") * own_z - margin + jnp.arange(array.shape[0], dtype=jnp.int32)
    pos_y = lax.axis_index("narrow") * own_y - margin + jnp.arange(array.shape[1], dtype=jnp.int32)
    valid_z = (pos_z >= 0) & (pos_z < own_z * lax.axis_size("wide"))
    valid_y = (pos_y >= 0) & (pos_y < own_y * lax.axis_size("narrow"))
    inside = valid_z[:, None, None] & valid_y[None, :, None]
    return jnp.where(inside, array, value)


def per_device(displacement, material, level_set):
    size_x = displacement.shape[2]
    size_y = displacement.shape[3]
    size_z = displacement.shape[4]
    padded = with_halo(displacement, (("wide", 2), ("narrow", 3)), 2)
    padded = jnp.pad(padded, ((0, 0), (0, 0), (0, 0), (0, 0), (2, 2)))
    val_z = apply_taps(padded, VAL_TAPS, 4, size_z)
    der_z = apply_taps(padded, DER_TAPS, 4, size_z)
    vv = apply_taps(val_z, VAL_TAPS, 3, size_y)
    vd = apply_taps(val_z, DER_TAPS, 3, size_y)
    dv = apply_taps(der_z, VAL_TAPS, 3, size_y)
    grad_x = apply_taps(vv, DER_TAPS, 2, size_x)
    grad_y = apply_taps(vd, VAL_TAPS, 2, size_x)
    grad_z = apply_taps(dv, VAL_TAPS, 2, size_x)
    stiffness = 0.2 + 0.8 * jnp.repeat(material.astype(jnp.float32), BZ, axis=2)
    energy = strain_energy(grad_x, grad_y, grad_z, stiffness)
    peak = lax.pmax(jnp.max(energy), ("wide", "narrow"))
    slab_velocity = jnp.transpose(energy / (peak + 1e-06) - 0.5, (2, 1, 0))
    velocity = lax.all_to_all(slab_velocity, "wide", split_axis=0, concat_axis=2, tiled=True)
    vel_wide, phi_wide = (
        with_halo(velocity, (("wide", 0), ("narrow", 1)), EXT_PASSES),
        with_halo(level_set, (("wide", 0), ("narrow", 1)), EXT_PASSES),
    )
    weight_wide = 1.0 / (1.0 + 4.0 * phi_wide * phi_wide)
    speed = vel_wide
    for step in range(EXT_PASSES):
        speed = ghost_fill(speed, EXT_PASSES - step, 0.0)
        weight_in = inner_region(weight_wide, step + 1)
        speed = weight_in * inner_region(vel_wide, step + 1) + (1.0 - weight_in) * neighbour_mean(
            speed
        )
    phi = level_set
    for step in range(HJ_STEPS):
        beside_all = with_halo(phi, (("wide", 0), ("narrow", 1)), 3)
        phi = march_step(ghost_fill(beside_all, 3, 1.0), speed)
    return (phi, speed)


def solution(mesh):
    return jax.shard_map(
        per_device,
        mesh=mesh,
        in_specs=(
            P(None, None, "wide", "narrow", None),
            P("wide", "narrow", None),
            P("wide", "narrow", None),
        ),
        out_specs=(P("wide", "narrow", None), P("wide", "narrow", None)),
        check_vma=False,
    )
```

profile of v0, /device:TPU:1, one launch (start us, length us, event | category | flops | bytes accessed | tf_op | source)
XLA Modules:
  0.0 449.2 jit_solution(12722956521881111135)
XLA Ops:
  3.4 4.8 %collective-permute-start.8 = (f32[3,3,2,32,384]{4,3,2,1,0:T(8,128)}, f32[3,3,2,32,384]{4,3,2,1,0:T(8,128)}, u32[]{:S(2)}, u32[]{:S(2)}) collective-permute-start(f32[3,3,2,32,384]{4,3,2,1,0:T(8,128)} %get-tuple-element.30), channel_id=1, source_target_pairs={{0,4},{4,8},{8,12},{12,16},{16,20},{20,24},{24,28},{1,5},{5,9},{9,... | collective-permute-start | bytes 2654216 | tf_op jit(solution)/shard_map/ppermute | solution.py:24
  23.6 22.8 %collective-permute-done.8 = f32[3,3,2,32,384]{4,3,2,1,0:T(8,128)} collective-permute-done((f32[3,3,2,32,384]{4,3,2,1,0:T(8,128)}, f32[3,3,2,32,384]{4,3,2,1,0:T(8,128)}, u32[]{:S(2)}, u32[]{:S(2)}) %collective-permute-start.8) | collective-permute-done | bytes 884768 | tf_op jit(solution)/shard_map/ppermute | solution.py:24
  49.1 5.7 %collective-permute-start.10 = (f32[3,3,20,2,384]{4,2,3,1,0:T(8,128)S(1)}, f32[3,3,20,2,384]{4,2,3,1,0:T(8,128)S(1)}, u32[]{:S(2)}, u32[]{:S(2)}) collective-permute-start(f32[3,3,20,2,384]{4,2,3,1,0:T(8,128)S(1)} %copy.238), channel_id=1, source_target_pairs={{0,1},{1,2},{2,3},{4,5},{5,6},{6,7},{8,9},{9,10},{10,11},{12,13},{... | collective-permute-start | bytes 1658888 | tf_op jit(solution)/shard_map/ppermute | solution.py:24
  57.0 5.4 %collective-permute-done.10 = f32[3,3,20,2,384]{4,2,3,1,0:T(8,128)S(1)} collective-permute-done((f32[3,3,20,2,384]{4,2,3,1,0:T(8,128)S(1)}, f32[3,3,20,2,384]{4,2,3,1,0:T(8,128)S(1)}, u32[]{:S(2)}, u32[]{:S(2)}) %collective-permute-start.10) | collective-permute-done | bytes 552992 | tf_op jit(solution)/shard_map/ppermute | solution.py:24
  67.2 9.1 %broadcast_multiply_fusion = (f32[3,3,20,36,384]{4,3,2,0,1:T(8,128)}, f32[3,3,20,36,384]{4,3,2,0,1:T(8,128)}) fusion(f32[3,3,20,2,384]{4,3,2,0,1:T(2,128)S(1)} %copy.241, f32[3,3,20,2,384]{4,3,2,0,1:T(2,128)S(1)} %copy.240, f32[3,3,2,32,384]{4,3,2,1,0:T(8,128)} %collective-permute-done.9, f32[3,3,16,32,384]{4,3,2,1,0:T(8,128)S(1)} %bitcast.57, ...), kind=kLoop, calls=%fused_computation.42 | loop fusion | flops 11888640 | bytes 29859840 | tf_op jit(solution)/shard_map/mul | solution.py:35
  76.3 44.3 %pad_slice_fusion.2 = (f32[3,3,20,36,384]{4,3,2,0,1:T(8,128)}, f32[3,3,20,36,384]{4,3,2,0,1:T(8,128)}, f32[3,3,20,36,384]{4,3,2,0,1:T(8,128)}, f32[3,3,20,36,384]{4,3,2,0,1:T(8,128)}) fusion(f32[3,3,20,36,384]{4,3,2,0,1:T(8,128)} %get-tuple-element.24), kind=kLoop, calls=%fused_computation.2 | loop fusion | flops 22394880 | bytes 49766400 | tf_op jit(solution)/shard_map/slice | solution.py:33
  120.7 18.9 %copy_add_fusion = f32[3,3,20,36,384]{4,3,2,1,0:T(8,128)} fusion(f32[3,3,20,36,384]{4,3,2,0,1:T(8,128)} %get-tuple-element.20, f32[3,3,20,36,384]{4,3,2,0,1:T(8,128)} %get-tuple-element.21, f32[3,3,20,36,384]{4,3,2,0,1:T(8,128)} %get-tuple-element.23, f32[3,3,20,36,384]{4,3,2,0,1:T(8,128)} %get-tuple-element.19), kind=kLoop, calls=%fused_computation.4 | loop fusion | flops 9953280 | bytes 49766400 | tf_op jit(solution)/shard_map/add | solution.py:35
  139.5 21.0 %fusion.60 = (f32[3,3,20,32,384]{4,3,2,1,0:T(8,128)}, f32[3,3,20,32,384]{4,3,2,1,0:T(8,128)}, f32[3,3,20,32,384]{4,3,2,1,0:T(8,128)}) fusion(f32[3,3,20,36,384]{4,3,2,1,0:T(8,128)} %copy_add_fusion), kind=kLoop, calls=%fused_computation.167 | loop fusion | bytes 53084160 | tf_op jit(solution)/shard_map/slice | solution.py:33
  160.6 17.0 %fusion.2 = f32[3,3,20,32,384]{4,3,2,1,0:T(8,128)} fusion(f32[3,3,20,36,384]{4,3,2,1,0:T(8,128)} %copy_add_fusion, f32[3,3,20,32,384]{4,3,2,1,0:T(8,128)} %get-tuple-element.18, f32[3,3,20,32,384]{4,3,2,1,0:T(8,128)} %get-tuple-element.17, f32[3,3,20,32,384]{4,3,2,1,0:T(8,128)} %get-tuple-element.16), kind=kLoop, calls=%fused_computation.12 | loop fusion | flops 15482880 | bytes 44236800 | tf_op jit(solution)/shard_map/add | solution.py:35
  177.6 13.7 %fusion.61 = (f32[3,3,16,32,384]{4,3,2,1,0:T(8,128)}, f32[3,3,16,32,384]{4,3,2,1,0:T(8,128)}, f32[3,3,16,32,384]{4,3,2,1,0:T(8,128)}) fusion(f32[3,3,20,32,384]{4,3,2,1,0:T(8,128)} %fusion.2), kind=kLoop, calls=%fused_computation.168 | loop fusion | bytes 42467328 | tf_op jit(solution)/shard_map/slice | solution.py:33
  191.3 9.2 %multiply_add_fusion.2 = (f32[3,3,20,32,384]{4,3,2,0,1:T(8,128)}, f32[3,3,20,32,384]{4,3,2,0,1:T(8,128)}) fusion(f32[3,3,20,36,384]{4,3,2,0,1:T(8,128)S(1)} %bitcast.55), kind=kLoop, calls=%fused_computation.20 | loop fusion | flops 30965760 | bytes 53084160 | tf_op jit(solution)/shard_map/add | solution.py:35
  200.5 23.4 %fusion.6 = (f32[3,3,16,32,384]{4,3,2,0,1:T(8,128)S(1)}, f32[3,3,16,32,384]{4,3,2,0,1:T(8,128)}) fusion(f32[3,3,20,32,384]{4,3,2,0,1:T(8,128)} %get-tuple-element.15, f32[3,3,20,32,384]{4,3,2,0,1:T(8,128)} %get-tuple-element.14), kind=kLoop, calls=%fused_computation.24 | loop fusion | flops 24772608 | bytes 70778880 | tf_op jit(solution)/shard_map/add | solution.py:35
  223.9 14.1 %fusion.5 = f32[3,3,16,32,384]{4,3,2,1,0:T(8,128)} fusion(f32[3,3,20,32,384]{4,3,2,1,0:T(8,128)} %fusion.2, f32[3,3,16,32,384]{4,3,2,1,0:T(8,128)} %get-tuple-element.27, f32[3,3,16,32,384]{4,3,2,1,0:T(8,128)} %get-tuple-element.26, f32[3,3,16,32,384]{4,3,2,1,0:T(8,128)} %get-tuple-element.25), kind=kLoop, calls=%fused_computation.22 | loop fusion | flops 12386304 | bytes 35389440 | tf_op jit(solution)/shard_map/add | solution.py:35
  238.0 4.9 %fusion.15 = f32[16,32,384]{2,1,0:T(8,128)S(1)} fusion(f32[3,3,16,32,384]{4,3,2,0,1:T(8,128)S(1)} %get-tuple-element.58, f32[3,3,16,32,384]{4,3,2,1,0:T(8,128)} %fusion.5, f32[3,3,16,32,384]{4,3,2,0,1:T(8,128)S(1)} %copy-done), kind=kLoop, calls=%fused_computation.59 | loop fusion | flops 14548992 | bytes 22020096 | tf_op jit(solution)/shard_map/reduce_sum | solution.py:49
  243.8 41.3 %pmax.7 = f32[]{:T(128)} all-reduce(f32[]{:T(128)} %get-tuple-element.12), channel_id=1, replica_groups=mesh['wide'=8,'narrow'=4] {'wide','narrow'}, use_global_device_ids=true, to_apply=%region_2.3 | all-reduce | flops 1 | bytes 8 | tf_op jit(solution)/shard_map/pmax | solution.py:136
  300.3 4.8 %collective-permute-start.6 = (f32[56,4,128]{2,1,0:T(4,128)}, f32[56,4,128]{2,1,0:T(4,128)}, u32[]{:S(2)}, u32[]{:S(2)}) collective-permute-start(f32[56,4,128]{2,1,0:T(4,128)} %get-tuple-element.36), channel_id=1, source_target_pairs={{0,1},{1,2},{2,3},{4,5},{5,6},{6,7},{8,9},{9,10},{10,11},{12,13},{... | collective-permute-start | bytes 344072 | tf_op jit(solution)/shard_map/ppermute | solution.py:24
  307.8 5.7 %all-to-all-done = f32[8,1,24576]{2,1,0:T(1,128)S(1)} async-done(((f32[8,1,24576]{2,1,0:T(1,128)}), f32[8,1,24576]{2,1,0:T(1,128)S(1)}, u32[]{:S(2)}, u32[]{:S(2)}) %all-to-all-start) | async-done | bytes 786464 | tf_op jit(solution)/shard_map/all_to_all | solution.py:138
  322.8 5.0 %fusion.64 = (f32[4,32,8,16]{0,2,3,1:T(8,128)}, f32[4,32,8,16]{0,2,3,1:T(8,128)}) fusion(f32[48,32,8,16]{0,2,3,1:T(8,128)} %bitcast.60), kind=kLoop, calls=%fused_computation.171 | loop fusion | bytes 262144 | tf_op jit(solution)/shard_map/slice | solution.py:25
  340.4 5.7 %collective-permute-start.2 = (f32[54,3,128]{2,1,0:T(4,128)}, f32[54,3,128]{2,1,0:T(4,128)}, u32[]{:S(2)}, u32[]{:S(2)}) collective-permute-start(f32[54,3,128]{2,1,0:T(4,128)} %get-tuple-element.44), channel_id=1, source_target_pairs={{0,1},{1,2},{2,3},{4,5},{5,6},{6,7},{8,9},{9,10},{10,11},{12,13},{... | collective-permute-start | bytes 248840 | tf_op jit(solution)/shard_map/ppermute | solution.py:24
  370.9 12.8 %slice_subtract_fusion.8 = (f32[48,32,128]{2,1,0:T(8,128)S(1)}, f32[48,32,128]{2,1,0:T(8,128)S(1)}) fusion(f32[54,38,128]{2,1,0:T(8,128)S(1)} %get-tuple-element.57, f32[48,32,133]{2,1,0:T(8,128)S(1)} %fusion.30, f32[48,37,128]{2,1,0:T(8,128)S(1)} %slice_subtract_fusion.2, f32[53,32,128]{2,1,0:T(8,128)S(1)} %slice_subtract_fusion.5, ...), kind=kLoop, calls=%fused_computation.135 | loop fusion | flops 83165184 | bytes 22257664 | tf_op jit(solution)/shard_map/sub | solution.py:99
  383.7 4.3 collective-permute-start.16
  398.0 4.1 collective-permute-done.19
  404.0 12.1 %slice_subtract_fusion.7 = f32[48,32,128]{2,1,0:T(8,128)S(1)} fusion(f32[54,38,128]{2,1,0:T(8,128)S(1)} %maximum_select_fusion.1, f32[48,32,133]{2,1,0:T(8,128)S(1)} %fusion.31, f32[48,37,128]{2,1,0:T(8,128)S(1)} %slice_subtract_fusion.1, f32[53,32,128]{2,1,0:T(8,128)S(1)} %slice_subtract_fusion.4, f32[48,32,128]{2,1,0:T(8,128)S(1)} %get-tuple-element.11), kind=kLoop, calls=%fused_computation.131 | loop fusion | flops 81199104 | bytes 16515072 | tf_op jit(solution)/shard_map/sub | solution.py:99
  436.1 12.8 %slice_subtract_fusion.6 = f32[48,32,128]{2,1,0:T(8,128)} fusion(f32[54,38,128]{2,1,0:T(8,128)S(1)} %maximum_select_fusion.2, f32[48,32,133]{2,1,0:T(8,128)S(1)} %fusion.32, f32[48,37,128]{2,1,0:T(8,128)S(1)} %slice_subtract_fusion, f32[53,32,128]{2,1,0:T(8,128)S(1)} %slice_subtract_fusion.3, f32[48,32,128]{2,1,0:T(8,128)S(1)} %get-tuple-element.11), kind=kLoop, calls=%fused_computation.130 | loop fusion | flops 81199104 | bytes 16515072 | tf_op jit(solution)/shard_map/sub | solution.py:99
  (130 shorter events, 123.9 us)
Async XLA Ops:
  3.4 42.9 %collective-permute-start.8 = (f32[3,3,2,32,384]{4,3,2,1,0:T(8,128)}, f32[3,3,2,32,384]{4,3,2,1,0:T(8,128)}, u32[]{:S(2)}, u32[]{:S(2)}) collective-permute-start(f32[3,3,2,32,384]{4,3,2,1,0:T(8,128)} %get-tuple-element.30), channel_id=1, source_target_pairs={{0,4},{4,8},{8,12},{12,16},{16,20},{20,24},{24,28},{1,5},{5,9},{9,... | collective-permute-start | bytes 2654216 | tf_op jit(solution)/shard_map/ppermute | solution.py:24
  8.3 38.1 %collective-permute-start.9 = (f32[3,3,2,32,384]{4,3,2,1,0:T(8,128)}, f32[3,3,2,32,384]{4,3,2,1,0:T(8,128)}, u32[]{:S(2)}, u32[]{:S(2)}) collective-permute-start(f32[3,3,2,32,384]{4,3,2,1,0:T(8,128)} %get-tuple-element.31), channel_id=1, source_target_pairs={{4,0},{8,4},{12,8},{16,12},{20,16},{24,20},{28,24},{5,1},{9,5},{13... | collective-permute-start | bytes 2654216 | tf_op jit(solution)/shard_map/ppermute | solution.py:27
  10.5 286.6 %collective-permute-start.4 = (f32[4,32,128]{2,1,0:T(8,128)S(1)}, f32[4,32,128]{2,1,0:T(8,128)S(1)}, u32[]{:S(2)}, u32[]{:S(2)}) collective-permute-start(f32[4,32,128]{2,1,0:T(8,128)S(1)} %get-tuple-element.51), channel_id=1, source_target_pairs={{0,4},{4,8},{8,12},{12,16},{16,20},{20,24},{24,28},{1,5},{5,9},{9,... | collective-permute-start | bytes 196616 | tf_op jit(solution)/shard_map/ppermute | solution.py:24
  15.9 280.5 %collective-permute-start = (f32[3,32,128]{2,1,0:T(8,128)}, f32[3,32,128]{2,1,0:T(8,128)S(1)}, u32[]{:S(2)}, u32[]{:S(2)}) collective-permute-start(f32[3,32,128]{2,1,0:T(8,128)} %get-tuple-element.55), channel_id=1, source_target_pairs={{0,4},{4,8},{8,12},{12,16},{16,20},{20,24},{24,28},{1,5},{5,9},{9,... | collective-permute-start | bytes 147464 | tf_op jit(solution)/shard_map/ppermute | solution.py:24
  19.1 280.3 %collective-permute-start.5 = (f32[4,32,128]{2,1,0:T(8,128)S(1)}, f32[4,32,128]{2,1,0:T(8,128)S(1)}, u32[]{:S(2)}, u32[]{:S(2)}) collective-permute-start(f32[4,32,128]{2,1,0:T(8,128)S(1)} %get-tuple-element.50), channel_id=1, source_target_pairs={{4,0},{8,4},{12,8},{16,12},{20,16},{24,20},{28,24},{5,1},{9,5},{13... | collective-permute-start | bytes 196616 | tf_op jit(solution)/shard_map/ppermute | solution.py:27
  49.1 13.3 %collective-permute-start.10 = (f32[3,3,20,2,384]{4,2,3,1,0:T(8,128)S(1)}, f32[3,3,20,2,384]{4,2,3,1,0:T(8,128)S(1)}, u32[]{:S(2)}, u32[]{:S(2)}) collective-permute-start(f32[3,3,20,2,384]{4,2,3,1,0:T(8,128)S(1)} %copy.238), channel_id=1, source_target_pairs={{0,1},{1,2},{2,3},{4,5},{5,6},{6,7},{8,9},{9,10},{10,11},{12,13},{... | collective-permute-start | bytes 1658888 | tf_op jit(solution)/shard_map/ppermute | solution.py:24
  54.9 12.0 %collective-permute-start.11 = (f32[3,3,20,2,384]{4,2,3,1,0:T(8,128)S(1)}, f32[3,3,20,2,384]{4,2,3,1,0:T(8,128)S(1)}, u32[]{:S(2)}, u32[]{:S(2)}) collective-permute-start(f32[3,3,20,2,384]{4,2,3,1,0:T(8,128)S(1)} %copy.239), channel_id=1, source_target_pairs={{1,0},{2,1},{3,2},{5,4},{6,5},{7,6},{9,8},{10,9},{11,10},{13,12},{... | collective-permute-start | bytes 1658888 | tf_op jit(solution)/shard_map/ppermute | solution.py:27
  62.4 244.8 %collective-permute-start.1 = (f32[3,32,128]{2,1,0:T(8,128)}, f32[3,32,128]{2,1,0:T(8,128)S(1)}, u32[]{:S(2)}, u32[]{:S(2)}) collective-permute-start(f32[3,32,128]{2,1,0:T(8,128)} %get-tuple-element.54), channel_id=1, source_target_pairs={{4,0},{8,4},{12,8},{16,12},{20,16},{24,20},{28,24},{5,1},{9,5},{13... | collective-permute-start | bytes 147464 | tf_op jit(solution)/shard_map/ppermute | solution.py:27
  291.0 22.5 %all-to-all-start = ((f32[8,1,24576]{2,1,0:T(1,128)}), f32[8,1,24576]{2,1,0:T(1,128)S(1)}, u32[]{:S(2)}, u32[]{:S(2)}) async-start(f32[8,1,24576]{2,1,0:T(1,128)} %reshape.225), calls=%async_computation | async-start | bytes 1572864 | tf_op jit(solution)/shard_map/all_to_all | solution.py:138
  300.3 57.1 %collective-permute-start.6 = (f32[56,4,128]{2,1,0:T(4,128)}, f32[56,4,128]{2,1,0:T(4,128)}, u32[]{:S(2)}, u32[]{:S(2)}) collective-permute-start(f32[56,4,128]{2,1,0:T(4,128)} %get-tuple-element.36), channel_id=1, source_target_pairs={{0,1},{1,2},{2,3},{4,5},{5,6},{6,7},{8,9},{9,10},{10,11},{12,13},{... | collective-permute-start | bytes 344072 | tf_op jit(solution)/shard_map/ppermute | solution.py:24
  305.1 54.4 %collective-permute-start.7 = (f32[56,4,128]{2,1,0:T(4,128)}, f32[56,4,128]{2,1,0:T(4,128)}, u32[]{:S(2)}, u32[]{:S(2)}) collective-permute-start(f32[56,4,128]{2,1,0:T(4,128)} %get-tuple-element.37), channel_id=1, source_target_pairs={{1,0},{2,1},{3,2},{5,4},{6,5},{7,6},{9,8},{10,9},{11,10},{13,12},{... | collective-permute-start | bytes 344072 | tf_op jit(solution)/shard_map/ppermute | solution.py:27
  330.6 21.1 %collective-permute-start.12 = (f32[4,32,128]{2,1,0:T(8,128)S(1)}, f32[4,32,128]{2,1,0:T(8,128)S(1)}, u32[]{:S(2)}, u32[]{:S(2)}) collective-permute-start(f32[4,32,128]{2,1,0:T(8,128)S(1)} %copy.271), channel_id=1, source_target_pairs={{0,4},{4,8},{8,12},{12,16},{16,20},{20,24},{24,28},{1,5},{5,9},{9,... | collective-permute-start | bytes 196616 | tf_op jit(solution)/shard_map/ppermute | solution.py:24
  337.4 16.3 %collective-permute-start.13 = (f32[4,32,128]{2,1,0:T(8,128)}, f32[4,32,128]{2,1,0:T(8,128)S(1)}, u32[]{:S(2)}, u32[]{:S(2)}) collective-permute-start(f32[4,32,128]{2,1,0:T(8,128)} %copy.273), channel_id=1, source_target_pairs={{4,0},{8,4},{12,8},{16,12},{20,16},{24,20},{28,24},{5,1},{9,5},{13... | collective-permute-start | bytes 196616 | tf_op jit(solution)/shard_map/ppermute | solution.py:27
  340.4 23.9 %collective-permute-start.2 = (f32[54,3,128]{2,1,0:T(4,128)}, f32[54,3,128]{2,1,0:T(4,128)}, u32[]{:S(2)}, u32[]{:S(2)}) collective-permute-start(f32[54,3,128]{2,1,0:T(4,128)} %get-tuple-element.44), channel_id=1, source_target_pairs={{0,1},{1,2},{2,3},{4,5},{5,6},{6,7},{8,9},{9,10},{10,11},{12,13},{... | collective-permute-start | bytes 248840 | tf_op jit(solution)/shard_map/ppermute | solution.py:24
  351.7 12.6 %collective-permute-start.3 = (f32[54,3,128]{2,1,0:T(4,128)}, f32[54,3,128]{2,1,0:T(4,128)S(1)}, u32[]{:S(2)}, u32[]{:S(2)}) collective-permute-start(f32[54,3,128]{2,1,0:T(4,128)} %get-tuple-element.45), channel_id=1, source_target_pairs={{1,0},{2,1},{3,2},{5,4},{6,5},{7,6},{9,8},{10,9},{11,10},{13,12},{... | collective-permute-start | bytes 248840 | tf_op jit(solution)/shard_map/ppermute | solution.py:27
  353.7 7.3 %collective-permute-start.14 = (f32[56,4,128]{2,1,0:T(4,128)S(1)}, f32[56,4,128]{2,1,0:T(4,128)S(1)}, u32[]{:S(2)}, u32[]{:S(2)}) collective-permute-start(f32[56,4,128]{2,1,0:T(4,128)S(1)} %get-tuple-element.38), channel_id=1, source_target_pairs={{0,1},{1,2},{2,3},{4,5},{5,6},{6,7},{8,9},{9,10},{10,11},{12,13},{... | collective-permute-start | bytes 344072 | tf_op jit(solution)/shard_map/ppermute | solution.py:24
  357.4 6.1 %collective-permute-start.15 = (f32[56,4,128]{2,1,0:T(4,128)S(1)}, f32[56,4,128]{2,1,0:T(4,128)S(1)}, u32[]{:S(2)}, u32[]{:S(2)}) collective-permute-start(f32[56,4,128]{2,1,0:T(4,128)S(1)} %get-tuple-element.39), channel_id=1, source_target_pairs={{1,0},{2,1},{3,2},{5,4},{6,5},{7,6},{9,8},{10,9},{11,10},{13,12},{... | collective-permute-start | bytes 344072 | tf_op jit(solution)/shard_map/ppermute | solution.py:27
  383.7 5.6 %collective-permute-start.16 = (f32[3,32,128]{2,1,0:T(8,128)S(1)}, f32[3,32,128]{2,1,0:T(8,128)S(1)}, u32[]{:S(2)}, u32[]{:S(2)}) collective-permute-start(f32[3,32,128]{2,1,0:T(8,128)S(1)} %get-tuple-element.48), channel_id=1, source_target_pairs={{0,4},{4,8},{8,12},{12,16},{16,20},{20,24},{24,28},{1,5},{5,9},{9,... | collective-permute-start | bytes 147464 | tf_op jit(solution)/shard_map/ppermute | solution.py:24
  387.9 4.8 %collective-permute-start.17 = (f32[3,32,128]{2,1,0:T(8,128)S(1)}, f32[3,32,128]{2,1,0:T(8,128)S(1)}, u32[]{:S(2)}, u32[]{:S(2)}) collective-permute-start(f32[3,32,128]{2,1,0:T(8,128)S(1)} %get-tuple-element.49), channel_id=1, source_target_pairs={{4,0},{8,4},{12,8},{16,12},{20,16},{24,20},{28,24},{5,1},{9,5},{13... | collective-permute-start | bytes 147464 | tf_op jit(solution)/shard_map/ppermute | solution.py:27
  392.8 5.2 %collective-permute-start.18 = (f32[54,3,128]{2,1,0:T(4,128)S(1)}, f32[54,3,128]{2,1,0:T(4,128)S(1)}, u32[]{:S(2)}, u32[]{:S(2)}) collective-permute-start(f32[54,3,128]{2,1,0:T(4,128)S(1)} %get-tuple-element.42), channel_id=1, source_target_pairs={{0,1},{1,2},{2,3},{4,5},{5,6},{6,7},{8,9},{9,10},{10,11},{12,13},{... | collective-permute-start | bytes 248840 | tf_op jit(solution)/shard_map/ppermute | solution.py:24
  396.1 6.1 %collective-permute-start.19 = (f32[54,3,128]{2,1,0:T(4,128)S(1)}, f32[54,3,128]{2,1,0:T(4,128)S(1)}, u32[]{:S(2)}, u32[]{:S(2)}) collective-permute-start(f32[54,3,128]{2,1,0:T(4,128)S(1)} %get-tuple-element.43), channel_id=1, source_target_pairs={{1,0},{2,1},{3,2},{5,4},{6,5},{7,6},{9,8},{10,9},{11,10},{13,12},{... | collective-permute-start | bytes 248840 | tf_op jit(solution)/shard_map/ppermute | solution.py:27
  416.2 5.1 %collective-permute-start.20 = (f32[3,32,128]{2,1,0:T(8,128)S(1)}, f32[3,32,128]{2,1,0:T(8,128)S(1)}, u32[]{:S(2)}, u32[]{:S(2)}) collective-permute-start(f32[3,32,128]{2,1,0:T(8,128)S(1)} %get-tuple-element.46), channel_id=1, source_target_pairs={{0,4},{4,8},{8,12},{12,16},{16,20},{20,24},{24,28},{1,5},{5,9},{9,... | collective-permute-start | bytes 147464 | tf_op jit(solution)/shard_map/ppermute | solution.py:24
  424.9 5.4 %collective-permute-start.22 = (f32[54,3,128]{2,1,0:T(4,128)S(1)}, f32[54,3,128]{2,1,0:T(4,128)S(1)}, u32[]{:S(2)}, u32[]{:S(2)}) collective-permute-start(f32[54,3,128]{2,1,0:T(4,128)S(1)} %get-tuple-element.40), channel_id=1, source_target_pairs={{0,1},{1,2},{2,3},{4,5},{5,6},{6,7},{8,9},{9,10},{10,11},{12,13},{... | collective-permute-start | bytes 248840 | tf_op jit(solution)/shard_map/ppermute | solution.py:24
  428.1 6.1 %collective-permute-start.23 = (f32[54,3,128]{2,1,0:T(4,128)S(1)}, f32[54,3,128]{2,1,0:T(4,128)S(1)}, u32[]{:S(2)}, u32[]{:S(2)}) collective-permute-start(f32[54,3,128]{2,1,0:T(4,128)S(1)} %get-tuple-element.41), channel_id=1, source_target_pairs={{1,0},{2,1},{3,2},{5,4},{6,5},{7,6},{9,8},{10,9},{11,10},{13,12},{... | collective-permute-start | bytes 248840 | tf_op jit(solution)/shard_map/ppermute | solution.py:27
  (12 other events, 251.8 us)
where the time goes:
time: 453 us; the launch traced here: 449 us
  other arithmetic  202 us (45%)
  local copies, waits for them, and re-layouts  75.7 us (17%)
  starting transfers between devices  74 us (16%)
  waiting for transfers between devices  54 us (12%)
  blocking collectives  41.3 us (9%)
    add x5, other arithmetic, apply_taps(): total + taps[k] * lax.slice_in_dim(padded, 1 + k, 1 + k + count, axis=axis)  82.6 us
    ppermute x12, starting transfers between devices, with_halo(): lax.ppermute(lax.slice_in_dim(block, block.shape[dim] - width, None, axis...  49.8 us
    slice x1, other arithmetic, apply_taps(): total = taps[0] * lax.slice_in_dim(padded, 1, 1 + count, axis=axis)  44.3 us
    pmax x1, blocking collectives, per_device(): peak = lax.pmax(jnp.max(energy), ('wide', 'narrow'))  41.3 us
    sub x3, other arithmetic, march_step(): centre - TIME_STEP * (jnp.maximum(speed, 0.0) * jnp.sqrt(grow_plus) + jnp...  37.7 us
    slice x2, local copies, waits for them, and re-layouts, apply_taps(): total = taps[0] * lax.slice_in_dim(padded, 1, 1 + count, axis=axis)  34.7 us
    ppermute x12, waiting for transfers between devices, with_halo(): lax.ppermute(lax.slice_in_dim(block, block.shape[dim] - width, None, axis...  28.3 us
    ppermute x12, starting transfers between devices, with_halo(): lax.ppermute(lax.slice_in_dim(block, 0, width, axis=dim), axis, backward)  20.2 us
  transfers between devices with their start and end apart: 25, of which 9 were waited for; matrix products, arithmetic and copies ran while one was open for 50% of the time, Pallas kernels for 0%

commit v1 on v0

--- a/solution.py
+++ b/solution.py
@@ -1,6 +1,10 @@
+import functools
+
 import jax
 import jax.numpy as jnp
 from jax import lax
+from jax.experimental import pallas as pl
+from jax.experimental.pallas import tpu as pltpu
 from jax.sharding import PartitionSpec as P
 
 BZ = 16
@@ -29,24 +33,160 @@
     return block
 
 
-def apply_taps(padded, taps, axis, count):
-    total = taps[0] * lax.slice_in_dim(padded, 1, 1 + count, axis=axis)
-    for k in range(1, 4):
-        total = total + taps[k] * lax.slice_in_dim(padded, 1 + k, 1 + k + count, axis=axis)
-    return total
-
-
-def strain_energy(grad_x, grad_y, grad_z, stiffness):
-    exx = grad_x[:, 0]
-    eyy = grad_y[:, 1]
-    ezz = grad_z[:, 2]
-    exy = 0.5 * (grad_y[:, 0] + grad_x[:, 1])
-    exz = 0.5 * (grad_z[:, 0] + grad_x[:, 2])
-    eyz = 0.5 * (grad_z[:, 1] + grad_y[:, 2])
-    trace = exx + eyy + ezz
-    square = exx * exx + eyy * eyy + ezz * ezz + 2.0 * (exy * exy + exz * exz + eyz * eyz)
-    density = SHEAR * square + 0.5 * LAME * trace * trace
-    return stiffness * jnp.sum(density, axis=0)
+def shift_from(block, axis, dim, width, up):
+    count = lax.axis_size(axis)
+    if up:
+        pairs = [(i, i + 1) for i in range(count - 1)]
+        part = lax.slice_in_dim(block, block.shape[dim] - width, None, axis=dim)
+    else:
+        pairs = [(i + 1, i) for i in range(count - 1)]
+        part = lax.slice_in_dim(block, 0, width, axis=dim)
+    return lax.ppermute(part, axis, pairs)
+
+
+def z_filters(u):
+    size = u.shape[-1]
+    lane = lax.broadcasted_iota(jnp.int32, u.shape, u.ndim - 1)
+    last = u.ndim - 1
+    before = jnp.where(lane == 0, 0.0, pltpu.roll(u, 1, last))
+    after = jnp.where(lane == size - 1, 0.0, pltpu.roll(u, size - 1, last))
+    second = jnp.where(lane >= size - 2, 0.0, pltpu.roll(u, size - 2, last))
+    val = VAL_TAPS[0] * (before + second) + VAL_TAPS[1] * (u + after)
+    der = DER_TAPS[3] * (second - before) + DER_TAPS[2] * (after - u)
+    return val, der
+
+
+def energy_kernel(own_ref, xh_ref, yh_ref, stiff_ref, out_ref, peak_ref, val_ref, der_ref):
+    load = pl.program_id(0)
+    size_x, size_y, size_z = own_ref.shape[2:]
+    rows = val_ref.shape[2]
+
+    def plane(c, p, body, tail):
+        val, der = z_filters(body)
+        val_ref[c, p, 0:size_y, :] = val
+        der_ref[c, p, 0:size_y, :] = der
+        val, der = z_filters(tail)
+        val_ref[c, p, size_y:rows, :] = val
+        der_ref[c, p, size_y:rows, :] = der
+
+    for c in range(3):
+        @pl.loop(0, size_x)
+        def _(p):
+            plane(c, p, own_ref[0, c, p], yh_ref[0, c, p])
+
+        @pl.loop(0, 3)
+        def _(q):
+            plane(c, size_x + q, xh_ref[0, c, q], yh_ref[0, c, size_x + q])
+
+    def taps_x(ref, c, idx, cols):
+        parts = [ref[c, i, :, cols] for i in idx]
+        return parts[0] + parts[3], parts[1] + parts[2], parts[3] - parts[0], parts[2] - parts[1]
+
+    def along_y(val_part, der_part):
+        total = None
+        for k, shift in enumerate((1, 0, rows - 1, rows - 2)):
+            term = None
+            if val_part is not None:
+                term = VAL_TAPS[k] * val_part
+            if der_part is not None:
+                extra = DER_TAPS[k] * der_part
+                term = extra if term is None else term + extra
+            if shift:
+                term = pltpu.roll(term, shift, 0)
+            total = term if total is None else total + term
+        return total[0:size_y]
+
+    chunk = 128
+
+    @pl.loop(0, size_x)
+    def _(p):
+        low = jnp.where(p == 0, size_x + 2, p - 1)
+        idx = (low, p, p + 1, p + 2)
+        for piece in range(size_z // chunk):
+            cols = pl.ds(piece * chunk, chunk)
+            fields = []
+            for c in range(3):
+                outer, inner, far, near = taps_x(val_ref, c, idx, cols)
+                vv = VAL_TAPS[0] * outer + VAL_TAPS[1] * inner
+                dv = DER_TAPS[3] * far + DER_TAPS[2] * near
+                outer, inner, _, _ = taps_x(der_ref, c, idx, cols)
+                vz = VAL_TAPS[0] * outer + VAL_TAPS[1] * inner
+                fields.append((vv, dv, vz))
+            exx = along_y(fields[0][1], None)
+            eyy = along_y(None, fields[1][0])
+            ezz = along_y(fields[2][2], None)
+            exy = 0.5 * along_y(fields[1][1], fields[0][0])
+            exz = 0.5 * along_y(fields[0][2] + fields[2][1], None)
+            eyz = 0.5 * along_y(fields[1][2], fields[2][0])
+            trace = exx + eyy + ezz
+            square = exx * exx + eyy * eyy + ezz * ezz + 2.0 * (exy * exy + exz * exz + eyz * eyz)
+            density = SHEAR * square + 0.5 * LAME * trace * trace
+
+            @pl.when(load == 0)
+            def _():
+                out_ref[p, :, cols] = density
+
+            @pl.when(load > 0)
+            def _():
+                out_ref[p, :, cols] = out_ref[p, :, cols] + density
+
+    @pl.when(load == pl.num_programs(0) - 1)
+    def _():
+        peak_ref[...] = jnp.zeros(peak_ref.shape, jnp.float32)
+
+        @pl.loop(0, size_x)
+        def _(p):
+            energy = stiff_ref[p] * out_ref[p]
+            out_ref[p] = energy
+            peak_ref[...] = jnp.maximum(peak_ref[...], energy)
+
+
+def slab_energy(displacement, material):
+    loads, comps, size_x, size_y, size_z = displacement.shape
+    low_y = shift_from(displacement, "narrow", 3, 1, True)
+    high_y = shift_from(displacement, "narrow", 3, 2, False)
+    filler = jnp.zeros((loads, comps, size_x, 5, size_z), jnp.float32)
+    tail = jnp.concatenate([high_y, filler, low_y], axis=3)
+    ends = jnp.concatenate(
+        [
+            jnp.concatenate([displacement[:, :, :2], displacement[:, :, -1:]], axis=2),
+            jnp.concatenate([tail[:, :, :2], tail[:, :, -1:]], axis=2),
+        ],
+        axis=3,
+    )
+    high_x = shift_from(ends, "wide", 2, 2, False)
+    low_x = shift_from(ends, "wide", 2, 1, True)
+    beside = jnp.concatenate([high_x, low_x], axis=2)
+    beside_own = beside[:, :, :, :size_y]
+    tail = jnp.concatenate([tail, beside[:, :, :, size_y:]], axis=2)
+    stiffness = 0.2 + 0.8 * jnp.repeat(material.astype(jnp.float32), BZ, axis=2)
+    planes = size_x + 3
+    rows = size_y + 8
+    energy, peak = pl.pallas_call(
+        energy_kernel,
+        grid=(loads,),
+        out_shape=(
+            jax.ShapeDtypeStruct((size_x, size_y, size_z), jnp.float32),
+            jax.ShapeDtypeStruct((size_y, size_z), jnp.float32),
+        ),
+        in_specs=[
+            pl.BlockSpec((1, comps, size_x, size_y, size_z), lambda i: (i, 0, 0, 0, 0)),
+            pl.BlockSpec((1, comps, 3, size_y, size_z), lambda i: (i, 0, 0, 0, 0)),
+            pl.BlockSpec((1, comps, planes, 8, size_z), lambda i: (i, 0, 0, 0, 0)),
+            pl.BlockSpec((size_x, size_y, size_z), lambda i: (0, 0, 0)),
+        ],
+        out_specs=(
+            pl.BlockSpec((size_x, size_y, size_z), lambda i: (0, 0, 0)),
+            pl.BlockSpec((size_y, size_z), lambda i: (0, 0)),
+        ),
+        scratch_shapes=[
+            pltpu.VMEM((comps, planes, rows, size_z), jnp.float32),
+            pltpu.VMEM((comps, planes, rows, size_z), jnp.float32),
+        ],
+        compiler_params=pltpu.CompilerParams(vmem_limit_bytes=40 << 20),
+        cost_estimate=pl.CostEstimate(flops=100000000, bytes_accessed=12000000, transcendentals=0),
+    )(displacement, beside_own, tail, stiffness)
+    return energy, jnp.max(peak)
 
 
 def neighbour_mean(padded):
@@ -118,24 +258,15 @@
 
 
 def per_device(displacement, material, level_set):
-    size_x = displacement.shape[2]
-    size_y = displacement.shape[3]
-    size_z = displacement.shape[4]
-    padded = with_halo(displacement, (("wide", 2), ("narrow", 3)), 2)
-    padded = jnp.pad(padded, ((0, 0), (0, 0), (0, 0), (0, 0), (2, 2)))
-    val_z = apply_taps(padded, VAL_TAPS, 4, size_z)
-    der_z = apply_taps(padded, DER_TAPS, 4, size_z)
-    vv = apply_taps(val_z, VAL_TAPS, 3, size_y)
-    vd = apply_taps(val_z, DER_TAPS, 3, size_y)
-    dv = apply_taps(der_z, VAL_TAPS, 3, size_y)
-    grad_x = apply_taps(vv, DER_TAPS, 2, size_x)
-    grad_y = apply_taps(vd, VAL_TAPS, 2, size_x)
-    grad_z = apply_taps(dv, VAL_TAPS, 2, size_x)
-    stiffness = 0.2 + 0.8 * jnp.repeat(material.astype(jnp.float32), BZ, axis=2)
-    energy = strain_energy(grad_x, grad_y, grad_z, stiffness)
-    peak = lax.pmax(jnp.max(energy), ("wide", "narrow"))
-    slab_velocity = jnp.transpose(energy / (peak + 1e-06) - 0.5, (2, 1, 0))
-    velocity = lax.all_to_all(slab_velocity, "wide", split_axis=0, concat_axis=2, tiled=True)
+    energy, own_peak = slab_energy(displacement, material)
+    devices = lax.axis_size("wide") * lax.axis_size("narrow")
+    peaks = lax.all_to_all(
+        jnp.full((devices, 1, 128), own_peak), ("wide", "narrow"), split_axis=0, concat_axis=0, tiled=True
+    )
+    moved = lax.all_to_all(
+        jnp.transpose(energy, (2, 1, 0)), "wide", split_axis=0, concat_axis=2, tiled=True
+    )
+    velocity = moved / (jnp.max(peaks) + 1e-06) - 0.5
     vel_wide, phi_wide = (
         with_halo(velocity, (("wide", 0), ("narrow", 1)), EXT_PASSES),
         with_halo(level_set, (("wide", 0), ("narrow", 1)), EXT_PASSES),

time: 453 us -> 275 us (0.61)
  other arithmetic: 202 us -> 60.2 us
  blocking collectives: 41.3 us -> 0 us
  local copies, waits for them, and re-layouts: 75.7 us -> 37.9 us
  Pallas kernels: 0 us -> 36.6 us
  starting transfers between devices: 74 us -> 79 us
    add x6 -> x1, other arithmetic: 83.6 us -> 0.03 us  [slab_energy(): stiffness = 0.2 + 0.8 * jnp.repeat(material.astype(jnp.float32), BZ, axis=2)]
    slice x1 -> x0, other arithmetic: 44.3 us -> none  [apply_taps(): total = taps[0] * lax.slice_in_dim(padded, 1, 1 + count, axis=axis)]
    pmax x1 -> x0, blocking collectives: 41.3 us -> none  [per_device(): peak = lax.pmax(jnp.max(energy), ('wide', 'narrow'))]
    pallas_call x0 -> x1, Pallas kernels: none -> 36.6 us  [slab_energy(): pl.pallas_call(energy_kernel, grid=(loads,), out_shape=(jax.ShapeDtypeStr...]
    ppermute x0 -> x4, waiting for transfers between devices: none -> 32.9 us  [shift_from(): return lax.ppermute(part, axis, pairs)]
    slice x2 -> x10, local copies, waits for them, and re-layouts: 34.7 us -> 6.17 us  [the longest x2 2.5 us: shift_from(): part = lax.slice_in_dim(block, 0, width, axis=dim)]
    ppermute x12 -> x10, waiting for transfers between devices: 28.3 us -> 0.03 us  [with_halo(): lax.ppermute(lax.slice_in_dim(block, block.shape[dim] - width, None, axis...]
    ppermute x12 -> x10, starting transfers between devices: 49.8 us -> 36.8 us  [with_halo(): lax.ppermute(lax.slice_in_dim(block, block.shape[dim] - width, None, axis...]
  transfers between devices with their start and end apart: 25 -> 26, of which waited for: 9 -> 9; matrix products, arithmetic and copies ran while one was open for 50% -> 16% of each run, Pallas kernels for 0% -> 13%
where the time goes in v1:
time: 275 us; the launch traced here: 274 us
  starting transfers between devices  79 us (29%)
  other arithmetic  60.2 us (22%)
  waiting for transfers between devices  58 us (21%)
  local copies, waits for them, and re-layouts  37.9 us (14%)
  Pallas kernels  36.6 us (13%)
    sub x3, other arithmetic, march_step(): centre - TIME_STEP * (jnp.maximum(speed, 0.0) * jnp.sqrt(grow_plus) + jnp...  37.7 us
    ppermute x10, starting transfers between devices, with_halo(): lax.ppermute(lax.slice_in_dim(block, block.shape[dim] - width, None, axis...  36.8 us
    pallas_call x1, Pallas kernels, slab_energy(): pl.pallas_call(energy_kernel, grid=(loads,), out_shape=(jax.ShapeDtypeStr...  36.6 us
    ppermute x4, waiting for transfers between devices, shift_from(): return lax.ppermute(part, axis, pairs)  32.9 us
    ppermute x10, waiting for transfers between devices, with_halo(): lax.ppermute(lax.slice_in_dim(block, 0, width, axis=dim), axis, backward)  17.8 us
    ppermute x10, starting transfers between devices, with_halo(): lax.ppermute(lax.slice_in_dim(block, 0, width, axis=dim), axis, backward)  17 us
    ppermute x4, starting transfers between devices, shift_from(): return lax.ppermute(part, axis, pairs)  12.5 us
    unnamed x26, local copies, waits for them, and re-layouts  10.3 us
  transfers between devices with their start and end apart: 26, of which 9 were waited for; matrix products, arithmetic and copies ran while one was open for 16% of the time, Pallas kernels for 13%

profile of v1, /device:TPU:1, one launch (start us, length us, event | category | flops | bytes accessed | tf_op | source)
XLA Modules:
  0.0 273.7 jit_solution(3995225932740083784)
XLA Ops:
  7.3 4.5 %collective-permute-start.9 = (f32[3,3,16,1,384]{4,3,2,1,0:T(1,128)}, f32[3,3,16,1,384]{4,3,2,1,0:T(1,128)}, u32[]{:S(2)}, u32[]{:S(2)}) collective-permute-start(f32[3,3,16,1,384]{4,3,2,1,0:T(1,128)} %slice.479), channel_id=1, source_target_pairs={{0,1},{1,2},{2,3},{4,5},{5,6},{6,7},{8,9},{9,10},{10,11},{12,13},{... | collective-permute-start | bytes 663560 | tf_op jit(solution)/shard_map/ppermute | solution.py:44
  16.3 3.8 %collective-permute-start = (f32[3,32,128]{2,1,0:T(8,128)}, f32[3,32,128]{2,1,0:T(8,128)}, u32[]{:S(2)}, u32[]{:S(2)}) collective-permute-start(f32[3,32,128]{2,1,0:T(8,128)} %get-tuple-element.39), channel_id=1, source_target_pairs={{0,4},{4,8},{8,12},{12,16},{16,20},{20,24},{24,28},{1,5},{5,9},{9,... | collective-permute-start | bytes 147464 | tf_op jit(solution)/shard_map/ppermute | solution.py:28
  29.8 4.6 %collective-permute-start.11 = (f32[3,3,1,40,384]{4,3,2,1,0:T(8,128)S(1)}, f32[3,3,1,40,384]{4,3,2,1,0:T(8,128)S(1)}, u32[]{:S(2)}, u32[]{:S(2)}) collective-permute-start(f32[3,3,1,40,384]{4,3,2,1,0:T(8,128)S(1)} %slice.611), channel_id=1, source_target_pairs={{0,4},{4,8},{8,12},{12,16},{16,20},{20,24},{24,28},{1,5},{5,9},{9,... | collective-permute-start | bytes 1658888 | tf_op jit(solution)/shard_map/ppermute | solution.py:44
  34.6 21.6 %collective-permute-done.10 = f32[3,3,2,40,384]{4,3,2,1,0:T(8,128)S(1)} collective-permute-done((f32[3,3,2,40,384]{4,3,2,1,0:T(8,128)S(1)}, f32[3,3,2,40,384]{4,3,2,1,0:T(8,128)S(1)}, u32[]{:S(2)}, u32[]{:S(2)}) %collective-permute-start.10) | collective-permute-done | bytes 1105952 | tf_op jit(solution)/shard_map/ppermute | solution.py:44
  57.8 11.3 %collective-permute-done.11 = f32[3,3,1,40,384]{4,3,2,1,0:T(8,128)S(1)} collective-permute-done((f32[3,3,1,40,384]{4,3,2,1,0:T(8,128)S(1)}, f32[3,3,1,40,384]{4,3,2,1,0:T(8,128)S(1)}, u32[]{:S(2)}, u32[]{:S(2)}) %collective-permute-start.11) | collective-permute-done | bytes 552992 | tf_op jit(solution)/shard_map/ppermute | solution.py:44
  71.0 36.6 %shard_map.50 = (f32[16,32,384]{2,1,0:T(8,128)S(1)}, f32[32,384]{1,0:T(8,128)S(1)}) custom-call(f32[3,3,16,32,384]{4,3,2,1,0:T(8,128)S(1)} %bitcast.16, f32[3,3,3,32,384]{4,3,2,1,0:T(8,128)S(1)} %slice.612.xh_ref, f32[3,3,19,8,384]{4,3,2,1,0:T(8,128)S(1)} %pad_maximum_fusion.yh_ref, f32[16,32,384]{2,1,0:T(8,128)S(1)} %copy.108.stiff_ref), custom_call_target="tpu_custom_call" | custom-call | flops 100000000 | bytes 12000000 | tf_op jit(solution)/shard_map/pallas_call | solution.py:165
  109.5 8.3 %all-to-all-start.1 = ((f32[32,1,128]{2,1,0:T(1,128)}), f32[32,1,128]{2,1,0:T(1,128)S(1)}, u32[]{:S(2)}, u32[]{:S(2)}) async-start(f32[32,1,128]{2,1,0:T(1,128)} %broadcast_in_dim.89), calls=%async_computation.1 | async-start | bytes 32768 | tf_op jit(solution)/shard_map/all_to_all | solution.py:263
  120.1 3.5 %reshape.203 = f32[8,1,24576]{2,1,0:T(1,128)} reshape(f32[384,16,32]{2,1,0:T(8,128)} %bitcast.21) | data formatting | bytes 1572864
  124.5 4.5 %all-to-all-start = ((f32[8,1,24576]{2,1,0:T(1,128)}), f32[8,1,24576]{2,1,0:T(1,128)S(1)}, u32[]{:S(2)}, u32[]{:S(2)}) async-start(f32[8,1,24576]{2,1,0:T(1,128)} %reshape.203), calls=%async_computation | async-start | bytes 1572864 | tf_op jit(solution)/shard_map/all_to_all | solution.py:266
  134.6 3.7 %collective-permute-start.6 = (f32[56,4,128]{2,1,0:T(4,128)}, f32[56,4,128]{2,1,0:T(4,128)}, u32[]{:S(2)}, u32[]{:S(2)}) collective-permute-start(f32[56,4,128]{2,1,0:T(4,128)} %get-tuple-element.20), channel_id=1, source_target_pairs={{0,1},{1,2},{2,3},{4,5},{5,6},{6,7},{8,9},{9,10},{10,11},{12,13},{... | collective-permute-start | bytes 344072 | tf_op jit(solution)/shard_map/ppermute | solution.py:28
  142.1 6.2 %all-to-all-done = f32[8,1,24576]{2,1,0:T(1,128)S(1)} async-done(((f32[8,1,24576]{2,1,0:T(1,128)}), f32[8,1,24576]{2,1,0:T(1,128)S(1)}, u32[]{:S(2)}, u32[]{:S(2)}) %all-to-all-start) | async-done | bytes 786464 | tf_op jit(solution)/shard_map/all_to_all | solution.py:266
  159.0 3.4 %collective-permute-start.12 = (f32[4,32,128]{2,1,0:T(8,128)}, f32[4,32,128]{2,1,0:T(8,128)S(1)}, u32[]{:S(2)}, u32[]{:S(2)}) collective-permute-start(f32[4,32,128]{2,1,0:T(8,128)} %copy.114), channel_id=1, source_target_pairs={{0,4},{4,8},{8,12},{12,16},{16,20},{20,24},{24,28},{1,5},{5,9},{9,... | collective-permute-start | bytes 196616 | tf_op jit(solution)/shard_map/ppermute | solution.py:28
  165.6 4.7 %collective-permute-start.2 = (f32[54,3,128]{2,1,0:T(4,128)}, f32[54,3,128]{2,1,0:T(4,128)}, u32[]{:S(2)}, u32[]{:S(2)}) collective-permute-start(f32[54,3,128]{2,1,0:T(4,128)} %get-tuple-element.28), channel_id=1, source_target_pairs={{0,1},{1,2},{2,3},{4,5},{5,6},{6,7},{8,9},{9,10},{10,11},{12,13},{... | collective-permute-start | bytes 248840 | tf_op jit(solution)/shard_map/ppermute | solution.py:28
  178.0 3.6 %collective-permute-start.14 = (f32[56,4,128]{2,1,0:T(4,128)S(1)}, f32[56,4,128]{2,1,0:T(4,128)S(1)}, u32[]{:S(2)}, u32[]{:S(2)}) collective-permute-start(f32[56,4,128]{2,1,0:T(4,128)S(1)} %get-tuple-element.22), channel_id=1, source_target_pairs={{0,1},{1,2},{2,3},{4,5},{5,6},{6,7},{8,9},{9,10},{10,11},{12,13},{... | collective-permute-start | bytes 344072 | tf_op jit(solution)/shard_map/ppermute | solution.py:28
  195.7 12.8 %slice_subtract_fusion.8 = (f32[48,32,128]{2,1,0:T(8,128)S(1)}, f32[48,32,128]{2,1,0:T(8,128)S(1)}) fusion(f32[54,38,128]{2,1,0:T(8,128)S(1)} %get-tuple-element.41, f32[48,32,133]{2,1,0:T(8,128)S(1)} %fusion.2, f32[48,37,128]{2,1,0:T(8,128)S(1)} %slice_subtract_fusion.2, f32[53,32,128]{2,1,0:T(8,128)S(1)} %slice_subtract_fusion.5, ...), kind=kLoop, calls=%fused_computation.83 | loop fusion | flops 83165184 | bytes 22257664 | tf_op jit(solution)/shard_map/sub | solution.py:239
  208.5 4.3 %collective-permute-start.16 = (f32[3,32,128]{2,1,0:T(8,128)S(1)}, f32[3,32,128]{2,1,0:T(8,128)S(1)}, u32[]{:S(2)}, u32[]{:S(2)}) collective-permute-start(f32[3,32,128]{2,1,0:T(8,128)S(1)} %get-tuple-element.32), channel_id=1, source_target_pairs={{0,4},{4,8},{8,12},{12,16},{16,20},{20,24},{24,28},{1,5},{5,9},{9,... | collective-permute-start | bytes 147464 | tf_op jit(solution)/shard_map/ppermute | solution.py:28
  214.1 3.5 %collective-permute-done.17 = f32[3,32,128]{2,1,0:T(8,128)S(1)} collective-permute-done((f32[3,32,128]{2,1,0:T(8,128)S(1)}, f32[3,32,128]{2,1,0:T(8,128)S(1)}, u32[]{:S(2)}, u32[]{:S(2)}) %collective-permute-start.17) | collective-permute-done | bytes 49184 | tf_op jit(solution)/shard_map/ppermute | solution.py:31
  222.9 4.1 %collective-permute-done.19 = f32[54,3,128]{2,1,0:T(4,128)S(1)} collective-permute-done((f32[54,3,128]{2,1,0:T(4,128)S(1)}, f32[54,3,128]{2,1,0:T(4,128)S(1)}, u32[]{:S(2)}, u32[]{:S(2)}) %collective-permute-start.19) | collective-permute-done | bytes 82976 | tf_op jit(solution)/shard_map/ppermute | solution.py:31
  228.9 12.1 %slice_subtract_fusion.7 = f32[48,32,128]{2,1,0:T(8,128)S(1)} fusion(f32[54,38,128]{2,1,0:T(8,128)S(1)} %maximum_select_fusion.1, f32[48,32,133]{2,1,0:T(8,128)S(1)} %fusion.3, f32[48,37,128]{2,1,0:T(8,128)S(1)} %slice_subtract_fusion.1, f32[53,32,128]{2,1,0:T(8,128)S(1)} %slice_subtract_fusion.4, f32[48,32,128]{2,1,0:T(8,128)S(1)} %get-tuple-element.15), kind=kLoop, calls=%fused_computation.79 | loop fusion | flops 81199104 | bytes 16515072 | tf_op jit(solution)/shard_map/sub | solution.py:239
  241.0 3.8 %collective-permute-start.20 = (f32[3,32,128]{2,1,0:T(8,128)S(1)}, f32[3,32,128]{2,1,0:T(8,128)S(1)}, u32[]{:S(2)}, u32[]{:S(2)}) collective-permute-start(f32[3,32,128]{2,1,0:T(8,128)S(1)} %get-tuple-element.30), channel_id=1, source_target_pairs={{0,4},{4,8},{8,12},{12,16},{16,20},{20,24},{24,28},{1,5},{5,9},{9,... | collective-permute-start | bytes 147464 | tf_op jit(solution)/shard_map/ppermute | solution.py:28
  246.1 3.5 %collective-permute-done.21 = f32[3,32,128]{2,1,0:T(8,128)S(1)} collective-permute-done((f32[3,32,128]{2,1,0:T(8,128)S(1)}, f32[3,32,128]{2,1,0:T(8,128)S(1)}, u32[]{:S(2)}, u32[]{:S(2)}) %collective-permute-start.21) | collective-permute-done | bytes 49184 | tf_op jit(solution)/shard_map/ppermute | solution.py:31
  249.7 3.2 %collective-permute-start.22 = (f32[54,3,128]{2,1,0:T(4,128)S(1)}, f32[54,3,128]{2,1,0:T(4,128)S(1)}, u32[]{:S(2)}, u32[]{:S(2)}) collective-permute-start(f32[54,3,128]{2,1,0:T(4,128)S(1)} %get-tuple-element.24), channel_id=1, source_target_pairs={{0,1},{1,2},{2,3},{4,5},{5,6},{6,7},{8,9},{9,10},{10,11},{12,13},{... | collective-permute-start | bytes 248840 | tf_op jit(solution)/shard_map/ppermute | solution.py:28
  255.1 3.9 %collective-permute-done.23 = f32[54,3,128]{2,1,0:T(4,128)S(1)} collective-permute-done((f32[54,3,128]{2,1,0:T(4,128)S(1)}, f32[54,3,128]{2,1,0:T(4,128)S(1)}, u32[]{:S(2)}, u32[]{:S(2)}) %collective-permute-start.23) | collective-permute-done | bytes 82976 | tf_op jit(solution)/shard_map/ppermute | solution.py:31
  260.9 12.8 %slice_subtract_fusion.6 = f32[48,32,128]{2,1,0:T(8,128)} fusion(f32[54,38,128]{2,1,0:T(8,128)S(1)} %maximum_select_fusion.2, f32[48,32,133]{2,1,0:T(8,128)S(1)} %fusion.4, f32[48,37,128]{2,1,0:T(8,128)S(1)} %slice_subtract_fusion, f32[53,32,128]{2,1,0:T(8,128)S(1)} %slice_subtract_fusion.3, f32[48,32,128]{2,1,0:T(8,128)S(1)} %get-tuple-element.15), kind=kLoop, calls=%fused_computation.78 | loop fusion | flops 81199104 | bytes 16515072 | tf_op jit(solution)/shard_map/sub | solution.py:239
  (128 shorter events, 87.2 us)
Async XLA Ops:
  3.1 22.7 %collective-permute-start.8 = (f32[3,3,16,2,384]{4,3,2,1,0:T(2,128)}, f32[3,3,16,2,384]{4,3,2,1,0:T(2,128)S(1)}, u32[]{:S(2)}, u32[]{:S(2)}) collective-permute-start(f32[3,3,16,2,384]{4,3,2,1,0:T(2,128)} %slice.478), channel_id=1, source_target_pairs={{1,0},{2,1},{3,2},{5,4},{6,5},{7,6},{9,8},{10,9},{11,10},{13,12},{... | collective-permute-start | bytes 1327112 | tf_op jit(solution)/shard_map/ppermute | solution.py:44
  7.3 18.4 %collective-permute-start.9 = (f32[3,3,16,1,384]{4,3,2,1,0:T(1,128)}, f32[3,3,16,1,384]{4,3,2,1,0:T(1,128)}, u32[]{:S(2)}, u32[]{:S(2)}) collective-permute-start(f32[3,3,16,1,384]{4,3,2,1,0:T(1,128)} %slice.479), channel_id=1, source_target_pairs={{0,1},{1,2},{2,3},{4,5},{5,6},{6,7},{8,9},{9,10},{10,11},{12,13},{... | collective-permute-start | bytes 663560 | tf_op jit(solution)/shard_map/ppermute | solution.py:44
  12.5 119.3 %collective-permute-start.4 = (f32[4,32,128]{2,1,0:T(8,128)}, f32[4,32,128]{2,1,0:T(8,128)S(1)}, u32[]{:S(2)}, u32[]{:S(2)}) collective-permute-start(f32[4,32,128]{2,1,0:T(8,128)} %get-tuple-element.35), channel_id=1, source_target_pairs={{0,4},{4,8},{8,12},{12,16},{16,20},{20,24},{24,28},{1,5},{5,9},{9,... | collective-permute-start | bytes 196616 | tf_op jit(solution)/shard_map/ppermute | solution.py:28
  16.3 114.1 %collective-permute-start = (f32[3,32,128]{2,1,0:T(8,128)}, f32[3,32,128]{2,1,0:T(8,128)}, u32[]{:S(2)}, u32[]{:S(2)}) collective-permute-start(f32[3,32,128]{2,1,0:T(8,128)} %get-tuple-element.39), channel_id=1, source_target_pairs={{0,4},{4,8},{8,12},{12,16},{16,20},{20,24},{24,28},{1,5},{5,9},{9,... | collective-permute-start | bytes 147464 | tf_op jit(solution)/shard_map/ppermute | solution.py:28
  20.0 112.8 %collective-permute-start.5 = (f32[4,32,128]{2,1,0:T(8,128)S(1)}, f32[4,32,128]{2,1,0:T(8,128)S(1)}, u32[]{:S(2)}, u32[]{:S(2)}) collective-permute-start(f32[4,32,128]{2,1,0:T(8,128)S(1)} %get-tuple-element.34), channel_id=1, source_target_pairs={{4,0},{8,4},{12,8},{16,12},{20,16},{24,20},{28,24},{5,1},{9,5},{13... | collective-permute-start | bytes 196616 | tf_op jit(solution)/shard_map/ppermute | solution.py:31
  28.2 28.0 %collective-permute-start.10 = (f32[3,3,2,40,384]{4,3,2,1,0:T(8,128)S(1)}, f32[3,3,2,40,384]{4,3,2,1,0:T(8,128)S(1)}, u32[]{:S(2)}, u32[]{:S(2)}) collective-permute-start(f32[3,3,2,40,384]{4,3,2,1,0:T(8,128)S(1)} %slice.610), channel_id=1, source_target_pairs={{4,0},{8,4},{12,8},{16,12},{20,16},{24,20},{28,24},{5,1},{9,5},{13... | collective-permute-start | bytes 3317768 | tf_op jit(solution)/shard_map/ppermute | solution.py:44
  29.8 39.4 %collective-permute-start.11 = (f32[3,3,1,40,384]{4,3,2,1,0:T(8,128)S(1)}, f32[3,3,1,40,384]{4,3,2,1,0:T(8,128)S(1)}, u32[]{:S(2)}, u32[]{:S(2)}) collective-permute-start(f32[3,3,1,40,384]{4,3,2,1,0:T(8,128)S(1)} %slice.611), channel_id=1, source_target_pairs={{0,4},{4,8},{8,12},{12,16},{16,20},{20,24},{24,28},{1,5},{5,9},{9,... | collective-permute-start | bytes 1658888 | tf_op jit(solution)/shard_map/ppermute | solution.py:44
  56.2 84.0 %collective-permute-start.1 = (f32[3,32,128]{2,1,0:T(8,128)S(1)}, f32[3,32,128]{2,1,0:T(8,128)S(1)}, u32[]{:S(2)}, u32[]{:S(2)}) collective-permute-start(f32[3,32,128]{2,1,0:T(8,128)S(1)} %copy-done.5), channel_id=1, source_target_pairs={{4,0},{8,4},{12,8},{16,12},{20,16},{24,20},{28,24},{5,1},{9,5},{13... | collective-permute-start | bytes 147464 | tf_op jit(solution)/shard_map/ppermute | solution.py:31
  109.5 15.0 %all-to-all-start.1 = ((f32[32,1,128]{2,1,0:T(1,128)}), f32[32,1,128]{2,1,0:T(1,128)S(1)}, u32[]{:S(2)}, u32[]{:S(2)}) async-start(f32[32,1,128]{2,1,0:T(1,128)} %broadcast_in_dim.89), calls=%async_computation.1 | async-start | bytes 32768 | tf_op jit(solution)/shard_map/all_to_all | solution.py:263
  124.5 23.8 %all-to-all-start = ((f32[8,1,24576]{2,1,0:T(1,128)}), f32[8,1,24576]{2,1,0:T(1,128)S(1)}, u32[]{:S(2)}, u32[]{:S(2)}) async-start(f32[8,1,24576]{2,1,0:T(1,128)} %reshape.203), calls=%async_computation | async-start | bytes 1572864 | tf_op jit(solution)/shard_map/all_to_all | solution.py:266
  134.6 47.1 %collective-permute-start.6 = (f32[56,4,128]{2,1,0:T(4,128)}, f32[56,4,128]{2,1,0:T(4,128)}, u32[]{:S(2)}, u32[]{:S(2)}) collective-permute-start(f32[56,4,128]{2,1,0:T(4,128)} %get-tuple-element.20), channel_id=1, source_target_pairs={{0,1},{1,2},{2,3},{4,5},{5,6},{6,7},{8,9},{9,10},{10,11},{12,13},{... | collective-permute-start | bytes 344072 | tf_op jit(solution)/shard_map/ppermute | solution.py:28
  138.2 45.6 %collective-permute-start.7 = (f32[56,4,128]{2,1,0:T(4,128)}, f32[56,4,128]{2,1,0:T(4,128)}, u32[]{:S(2)}, u32[]{:S(2)}) collective-permute-start(f32[56,4,128]{2,1,0:T(4,128)} %get-tuple-element.21), channel_id=1, source_target_pairs={{1,0},{2,1},{3,2},{5,4},{6,5},{7,6},{9,8},{10,9},{11,10},{13,12},{... | collective-permute-start | bytes 344072 | tf_op jit(solution)/shard_map/ppermute | solution.py:31
  159.0 16.9 %collective-permute-start.12 = (f32[4,32,128]{2,1,0:T(8,128)}, f32[4,32,128]{2,1,0:T(8,128)S(1)}, u32[]{:S(2)}, u32[]{:S(2)}) collective-permute-start(f32[4,32,128]{2,1,0:T(8,128)} %copy.114), channel_id=1, source_target_pairs={{0,4},{4,8},{8,12},{12,16},{16,20},{20,24},{24,28},{1,5},{5,9},{9,... | collective-permute-start | bytes 196616 | tf_op jit(solution)/shard_map/ppermute | solution.py:28
  162.5 15.5 %collective-permute-start.13 = (f32[4,32,128]{2,1,0:T(8,128)S(1)}, f32[4,32,128]{2,1,0:T(8,128)S(1)}, u32[]{:S(2)}, u32[]{:S(2)}) collective-permute-start(f32[4,32,128]{2,1,0:T(8,128)S(1)} %copy.115), channel_id=1, source_target_pairs={{4,0},{8,4},{12,8},{16,12},{20,16},{24,20},{28,24},{5,1},{9,5},{13... | collective-permute-start | bytes 196616 | tf_op jit(solution)/shard_map/ppermute | solution.py:31
  165.6 23.1 %collective-permute-start.2 = (f32[54,3,128]{2,1,0:T(4,128)}, f32[54,3,128]{2,1,0:T(4,128)}, u32[]{:S(2)}, u32[]{:S(2)}) collective-permute-start(f32[54,3,128]{2,1,0:T(4,128)} %get-tuple-element.28), channel_id=1, source_target_pairs={{0,1},{1,2},{2,3},{4,5},{5,6},{6,7},{8,9},{9,10},{10,11},{12,13},{... | collective-permute-start | bytes 248840 | tf_op jit(solution)/shard_map/ppermute | solution.py:28
  175.9 12.8 %collective-permute-start.3 = (f32[54,3,128]{2,1,0:T(4,128)}, f32[54,3,128]{2,1,0:T(4,128)S(1)}, u32[]{:S(2)}, u32[]{:S(2)}) collective-permute-start(f32[54,3,128]{2,1,0:T(4,128)} %get-tuple-element.29), channel_id=1, source_target_pairs={{1,0},{2,1},{3,2},{5,4},{6,5},{7,6},{9,8},{10,9},{11,10},{13,12},{... | collective-permute-start | bytes 248840 | tf_op jit(solution)/shard_map/ppermute | solution.py:31
  178.0 7.0 %collective-permute-start.14 = (f32[56,4,128]{2,1,0:T(4,128)S(1)}, f32[56,4,128]{2,1,0:T(4,128)S(1)}, u32[]{:S(2)}, u32[]{:S(2)}) collective-permute-start(f32[56,4,128]{2,1,0:T(4,128)S(1)} %get-tuple-element.22), channel_id=1, source_target_pairs={{0,1},{1,2},{2,3},{4,5},{5,6},{6,7},{8,9},{9,10},{10,11},{12,13},{... | collective-permute-start | bytes 344072 | tf_op jit(solution)/shard_map/ppermute | solution.py:28
  181.7 6.1 %collective-permute-start.15 = (f32[56,4,128]{2,1,0:T(4,128)S(1)}, f32[56,4,128]{2,1,0:T(4,128)S(1)}, u32[]{:S(2)}, u32[]{:S(2)}) collective-permute-start(f32[56,4,128]{2,1,0:T(4,128)S(1)} %get-tuple-element.23), channel_id=1, source_target_pairs={{1,0},{2,1},{3,2},{5,4},{6,5},{7,6},{9,8},{10,9},{11,10},{13,12},{... | collective-permute-start | bytes 344072 | tf_op jit(solution)/shard_map/ppermute | solution.py:31
  208.5 5.6 %collective-permute-start.16 = (f32[3,32,128]{2,1,0:T(8,128)S(1)}, f32[3,32,128]{2,1,0:T(8,128)S(1)}, u32[]{:S(2)}, u32[]{:S(2)}) collective-permute-start(f32[3,32,128]{2,1,0:T(8,128)S(1)} %get-tuple-element.32), channel_id=1, source_target_pairs={{0,4},{4,8},{8,12},{12,16},{16,20},{20,24},{24,28},{1,5},{5,9},{9,... | collective-permute-start | bytes 147464 | tf_op jit(solution)/shard_map/ppermute | solution.py:28
  217.7 5.2 %collective-permute-start.18 = (f32[54,3,128]{2,1,0:T(4,128)S(1)}, f32[54,3,128]{2,1,0:T(4,128)S(1)}, u32[]{:S(2)}, u32[]{:S(2)}) collective-permute-start(f32[54,3,128]{2,1,0:T(4,128)S(1)} %get-tuple-element.26), channel_id=1, source_target_pairs={{0,1},{1,2},{2,3},{4,5},{5,6},{6,7},{8,9},{9,10},{10,11},{12,13},{... | collective-permute-start | bytes 248840 | tf_op jit(solution)/shard_map/ppermute | solution.py:28
  220.9 6.1 %collective-permute-start.19 = (f32[54,3,128]{2,1,0:T(4,128)S(1)}, f32[54,3,128]{2,1,0:T(4,128)S(1)}, u32[]{:S(2)}, u32[]{:S(2)}) collective-permute-start(f32[54,3,128]{2,1,0:T(4,128)S(1)} %get-tuple-element.27), channel_id=1, source_target_pairs={{1,0},{2,1},{3,2},{5,4},{6,5},{7,6},{9,8},{10,9},{11,10},{13,12},{... | collective-permute-start | bytes 248840 | tf_op jit(solution)/shard_map/ppermute | solution.py:31
  241.0 5.1 %collective-permute-start.20 = (f32[3,32,128]{2,1,0:T(8,128)S(1)}, f32[3,32,128]{2,1,0:T(8,128)S(1)}, u32[]{:S(2)}, u32[]{:S(2)}) collective-permute-start(f32[3,32,128]{2,1,0:T(8,128)S(1)} %get-tuple-element.30), channel_id=1, source_target_pairs={{0,4},{4,8},{8,12},{12,16},{16,20},{20,24},{24,28},{1,5},{5,9},{9,... | collective-permute-start | bytes 147464 | tf_op jit(solution)/shard_map/ppermute | solution.py:28
  249.7 5.4 %collective-permute-start.22 = (f32[54,3,128]{2,1,0:T(4,128)S(1)}, f32[54,3,128]{2,1,0:T(4,128)S(1)}, u32[]{:S(2)}, u32[]{:S(2)}) collective-permute-start(f32[54,3,128]{2,1,0:T(4,128)S(1)} %get-tuple-element.24), channel_id=1, source_target_pairs={{0,1},{1,2},{2,3},{4,5},{5,6},{6,7},{8,9},{9,10},{10,11},{12,13},{... | collective-permute-start | bytes 248840 | tf_op jit(solution)/shard_map/ppermute | solution.py:28
  252.9 6.1 %collective-permute-start.23 = (f32[54,3,128]{2,1,0:T(4,128)S(1)}, f32[54,3,128]{2,1,0:T(4,128)S(1)}, u32[]{:S(2)}, u32[]{:S(2)}) collective-permute-start(f32[54,3,128]{2,1,0:T(4,128)S(1)} %get-tuple-element.25), channel_id=1, source_target_pairs={{1,0},{2,1},{3,2},{5,4},{6,5},{7,6},{9,8},{10,9},{11,10},{13,12},{... | collective-permute-start | bytes 248840 | tf_op jit(solution)/shard_map/ppermute | solution.py:31
  (14 other events, 174.9 us)

commit v2 on v1

--- a/solution.py
+++ b/solution.py
@@ -18,19 +18,6 @@
 TIME_STEP = 0.3
 VAL_TAPS = (1.0 / 48.0, 23.0 / 48.0, 23.0 / 48.0, 1.0 / 48.0)
 DER_TAPS = (-1.0 / 8.0, -5.0 / 8.0, 5.0 / 8.0, 1.0 / 8.0)
-
-
-def with_halo(block, sides, width):
-    for axis, dim in sides:
-        count = lax.axis_size(axis)
-        forward = [(i, i + 1) for i in range(count - 1)]
-        backward = [(target, source) for source, target in forward]
-        low = lax.ppermute(
-            lax.slice_in_dim(block, block.shape[dim] - width, None, axis=dim), axis, forward
-        )
-        high = lax.ppermute(lax.slice_in_dim(block, 0, width, axis=dim), axis, backward)
-        block = jnp.concatenate([low, block, high], axis=dim)
-    return block
 
 
 def shift_from(block, axis, dim, width, up):
@@ -141,7 +128,7 @@
             peak_ref[...] = jnp.maximum(peak_ref[...], energy)
 
 
-def slab_energy(displacement, material):
+def slab_energy(displacement, material, early):
     loads, comps, size_x, size_y, size_z = displacement.shape
     low_y = shift_from(displacement, "narrow", 3, 1, True)
     high_y = shift_from(displacement, "narrow", 3, 2, False)
@@ -160,6 +147,7 @@
     beside_own = beside[:, :, :, :size_y]
     tail = jnp.concatenate([tail, beside[:, :, :, size_y:]], axis=2)
     stiffness = 0.2 + 0.8 * jnp.repeat(material.astype(jnp.float32), BZ, axis=2)
+    beside_own, tail, early = lax.optimization_barrier((beside_own, tail, early))
     planes = size_x + 3
     rows = size_y + 8
     energy, peak = pl.pallas_call(
@@ -186,104 +174,206 @@
         compiler_params=pltpu.CompilerParams(vmem_limit_bytes=40 << 20),
         cost_estimate=pl.CostEstimate(flops=100000000, bytes_accessed=12000000, transcendentals=0),
     )(displacement, beside_own, tail, stiffness)
-    return energy, jnp.max(peak)
-
-
-def neighbour_mean(padded):
-    wider = jnp.pad(padded, ((0, 0), (0, 0), (1, 1)))
-    total = wider[2:, 1:-1, 1:-1] + wider[:-2, 1:-1, 1:-1]
-    total = total + wider[1:-1, 2:, 1:-1] + wider[1:-1, :-2, 1:-1]
-    total = total + wider[1:-1, 1:-1, 2:] + wider[1:-1, 1:-1, :-2]
-    return total * (1.0 / 6.0)
-
-
-def weno_side(v1, v2, v3, v4, v5):
-    p_one = v1 / 3.0 - 7.0 * v2 / 6.0 + 11.0 * v3 / 6.0
-    p_two = -v2 / 6.0 + 5.0 * v3 / 6.0 + v4 / 3.0
-    p_three = v3 / 3.0 + 5.0 * v4 / 6.0 - v5 / 6.0
-    b_one = 13.0 / 12.0 * (v1 - 2.0 * v2 + v3) ** 2 + 0.25 * (v1 - 4.0 * v2 + 3.0 * v3) ** 2
-    b_two = 13.0 / 12.0 * (v2 - 2.0 * v3 + v4) ** 2 + 0.25 * (v2 - v4) ** 2
-    b_three = 13.0 / 12.0 * (v3 - 2.0 * v4 + v5) ** 2 + 0.25 * (3.0 * v3 - 4.0 * v4 + v5) ** 2
-    a_one = 0.1 / (WENO_EPS + b_one) ** 2
-    a_two = 0.6 / (WENO_EPS + b_two) ** 2
-    a_three = 0.3 / (WENO_EPS + b_three) ** 2
-    return (a_one * p_one + a_two * p_two + a_three * p_three) / (a_one + a_two + a_three)
-
-
-def march_step(padded, speed):
-    wider = jnp.pad(padded, ((0, 0), (0, 0), (3, 3)), constant_values=1.0)
-    size_z = padded.shape[0] - 6
-    size_y = padded.shape[1] - 6
-    size_x = padded.shape[2]
-    centre = wider[3 : 3 + size_z, 3 : 3 + size_y, 3 : 3 + size_x]
-    lines = (
-        wider[:, 3 : 3 + size_y, 3 : 3 + size_x],
-        wider[3 : 3 + size_z, :, 3 : 3 + size_x],
-        wider[3 : 3 + size_z, 3 : 3 + size_y, :],
-    )
-    grow_plus = None
-    grow_minus = None
-    for axis in range(3):
-        line = lines[axis]
-        count = centre.shape[axis]
-        diffs = lax.slice_in_dim(line, 1, count + 6, axis=axis) - lax.slice_in_dim(
-            line, 0, count + 5, axis=axis
-        )
-        parts = [lax.slice_in_dim(diffs, k, k + count, axis=axis) for k in range(6)]
-        minus = weno_side(parts[0], parts[1], parts[2], parts[3], parts[4])
-        plus = weno_side(parts[5], parts[4], parts[3], parts[2], parts[1])
-        term_p = jnp.maximum(jnp.maximum(minus, 0.0) ** 2, jnp.minimum(plus, 0.0) ** 2)
-        term_m = jnp.maximum(jnp.minimum(minus, 0.0) ** 2, jnp.maximum(plus, 0.0) ** 2)
-        grow_plus = term_p if grow_plus is None else grow_plus + term_p
-        grow_minus = term_m if grow_minus is None else grow_minus + term_m
-    return centre - TIME_STEP * (
-        jnp.maximum(speed, 0.0) * jnp.sqrt(grow_plus)
-        + jnp.minimum(speed, 0.0) * jnp.sqrt(grow_minus)
-    )
-
-
-def inner_region(array, margin):
-    return array[margin : array.shape[0] - margin, margin : array.shape[1] - margin]
-
-
-def ghost_fill(array, margin, value):
-    own_z = array.shape[0] - 2 * margin
-    own_y = array.shape[1] - 2 * margin
-    pos_z = lax.axis_index("wide") * own_z - margin + jnp.arange(array.shape[0], dtype=jnp.int32)
-    pos_y = lax.axis_index("narrow") * own_y - margin + jnp.arange(array.shape[1], dtype=jnp.int32)
-    valid_z = (pos_z >= 0) & (pos_z < own_z * lax.axis_size("wide"))
-    valid_y = (pos_y >= 0) & (pos_y < own_y * lax.axis_size("narrow"))
-    inside = valid_z[:, None, None] & valid_y[None, :, None]
-    return jnp.where(inside, array, value)
+    return energy, jnp.max(peak), early
+
+
+def weno_pair(d):
+    e = [d[k + 1] - d[k] for k in range(5)]
+    s = [e[k + 1] - e[k] for k in range(4)]
+    bend = [(13.0 / 12.0) * s[k] * s[k] for k in range(4)]
+    twice = [None] + [2.0 * e[k] for k in (1, 2, 3)]
+    sixth = [None] + [(1.0 / 6.0) * e[k] for k in (1, 2, 3)]
+    third = (1.0 / 3.0) * e[2]
+
+    def blend(base, b_one, t_one, b_two, t_two, b_three, t_three, r_one, r_two, r_three):
+        a = WENO_EPS + b_one + 0.25 * t_one * t_one
+        b = WENO_EPS + b_two + 0.25 * t_two * t_two
+        c = WENO_EPS + b_three + 0.25 * t_three * t_three
+        a = a * a
+        b = b * b
+        c = c * c
+        w_one = 0.1 * (b * c)
+        w_two = 0.6 * (a * c)
+        w_three = 0.3 * (a * b)
+        return base + (w_one * r_one + w_two * r_two + w_three * r_three) / (w_one + w_two + w_three)
+
+    minus = blend(
+        d[2],
+        bend[0], s[0] + twice[1],
+        bend[1], e[1] + e[2],
+        bend[2], s[2] - twice[2],
+        (5.0 / 6.0) * e[1] - (1.0 / 3.0) * e[0],
+        sixth[1] + third,
+        2.0 * third - sixth[3],
+    )
+    plus = blend(
+        d[3],
+        bend[3], s[3] - twice[3],
+        bend[2], e[2] + e[3],
+        bend[1], s[1] + twice[2],
+        (1.0 / 3.0) * e[4] - (5.0 / 6.0) * e[3],
+        -(sixth[3] + third),
+        sixth[1] - 2.0 * third,
+    )
+    return minus, plus
+
+
+def lane_shift(u, offset, ghost):
+    if offset == 0:
+        return u
+    size = u.shape[-1]
+    lane = lax.broadcasted_iota(jnp.int32, u.shape, u.ndim - 1)
+    moved = pltpu.roll(u, (-offset) % size, u.ndim - 1)
+    outside = lane >= size - offset if offset > 0 else lane < -offset
+    return jnp.where(outside, ghost, moved)
+
+
+MARGIN = 3 * (HJ_STEPS - 1) + EXT_PASSES
+SIDE = -(-MARGIN // 8) * 8 + 8
+
+
+CHUNK = 8
+
+
+def march_kernel(
+    place, peak, vel_own, vel_low, vel_high, phi_own, phi_low, phi_high,
+    next_ref, speed_ref, pull, keep, one, two, first, second,
+):
+    deep, rows, size_x = pull.shape
+    own_y = rows - 2 * SIDE
+    own_z = deep - 2 * MARGIN
+    scale = peak[0] + 1e-06
+
+    def settle(z, lo, values, ghost):
+        here = place[0] + z
+        shape = values.shape
+        row = lax.broadcasted_iota(jnp.int32, shape, 0) + (lo + place[2])
+        lowest = jnp.where((here >= 0) & (here < place[1]), 0, place[3])
+        return jnp.where((row >= lowest) & (row < place[3]), values, ghost)
+
+    def window(margin):
+        lo = (SIDE - margin) // 8 * 8
+        return lo, rows - lo
+
+    @pl.loop(0, deep)
+    def _(z):
+        def fill(lo, size, energy, phi):
+            at = pl.ds(lo, size)
+            velocity = energy / scale - 0.5
+            weight = 1.0 / (1.0 + 4.0 * phi * phi)
+            pull[z, at, :] = weight * velocity
+            keep[z, at, :] = (1.0 - weight) * (1.0 / 6.0)
+            one[z, at, :] = settle(z, lo, velocity, 0.0)
+            first[z, at, :] = settle(z, lo, phi, 1.0)
+
+        fill(SIDE - MARGIN, MARGIN, vel_low[z], phi_low[z])
+        fill(SIDE, own_y, vel_own[z], phi_own[z])
+        fill(SIDE + own_y, MARGIN, vel_high[z], phi_high[z])
+
+    source, target = one, two
+    for step in range(EXT_PASSES):
+        margin = MARGIN - 1 - step
+        lo, hi = window(margin)
+
+        def extend(z, source=source, target=target, lo=lo, hi=hi):
+            for start in range(lo, hi, 16):
+                at = pl.ds(start, 16)
+                mid = source[z, at, :]
+                total = source[z - 1, at, :] + source[z + 1, at, :]
+                total = total + (source[z, pl.ds(start - 1, 16), :] + source[z, pl.ds(start + 1, 16), :])
+                total = total + (lane_shift(mid, 1, 0.0) + lane_shift(mid, -1, 0.0))
+                value = pull[z, at, :] + keep[z, at, :] * total
+                target[z, at, :] = settle(z, start, value, 0.0)
+
+        pl.loop(step + 1, deep - step - 1)(extend)
+        source, target = target, source
+    speed = source
+
+    source, target = first, second
+    for step in range(HJ_STEPS):
+        margin = 3 * (HJ_STEPS - 1 - step)
+        lo, hi = window(margin)
+        final = step == HJ_STEPS - 1
+
+        def march(z, source=source, target=target, lo=lo, hi=hi, final=final):
+            for start in range(lo, hi, CHUNK):
+                at = pl.ds(start, CHUNK)
+                mid = source[z, at, :]
+                lines = (
+                    [source[z + k, at, :] for k in range(-3, 4)],
+                    [source[z, pl.ds(start + k, CHUNK), :] for k in range(-3, 4)],
+                    [lane_shift(mid, k, 1.0) for k in range(-3, 4)],
+                )
+                grow_plus = None
+                grow_minus = None
+                for line in lines:
+                    minus, plus = weno_pair([line[k + 1] - line[k] for k in range(6)])
+                    up = jnp.maximum(jnp.maximum(minus, 0.0), -jnp.minimum(plus, 0.0))
+                    down = jnp.maximum(-jnp.minimum(minus, 0.0), jnp.maximum(plus, 0.0))
+                    grow_plus = up * up if grow_plus is None else grow_plus + up * up
+                    grow_minus = down * down if grow_minus is None else grow_minus + down * down
+                rate = speed[z, at, :]
+                growth = jnp.sqrt(jnp.where(rate > 0.0, grow_plus, grow_minus))
+                value = mid - TIME_STEP * (rate * growth)
+                if final:
+                    next_ref[z - MARGIN, pl.ds(start - SIDE, CHUNK), :] = value
+                    speed_ref[z - MARGIN, pl.ds(start - SIDE, CHUNK), :] = rate
+                else:
+                    target[z, at, :] = settle(z, start, value, 1.0)
+
+        pl.loop(MARGIN - margin, MARGIN + own_z + margin)(march)
+        source, target = target, source
+
+
+def rows_beside(block, width):
+    low = shift_from(block, "narrow", 1, width, True)
+    high = shift_from(block, "narrow", 1, width, False)
+    return block, low, high
+
+
+def march(velocity, phi, peak, own_z, own_y):
+    deep, _, size_x = phi[0].shape
+    place = jnp.stack(
+        [
+            lax.axis_index("wide") * own_z - MARGIN,
+            lax.axis_size("wide") * own_z,
+            lax.axis_index("narrow") * own_y - SIDE,
+            lax.axis_size("narrow") * own_y,
+        ]
+    ).astype(jnp.int32)
+    result = jax.ShapeDtypeStruct((own_z, own_y, size_x), jnp.float32)
+    smem = pl.BlockSpec(memory_space=pltpu.SMEM)
+    vmem = pl.BlockSpec(memory_space=pltpu.VMEM)
+    return pl.pallas_call(
+        march_kernel,
+        out_shape=(result, result),
+        in_specs=[smem, smem] + [vmem] * 6,
+        out_specs=(vmem, vmem),
+        scratch_shapes=[pltpu.VMEM((deep, own_y + 2 * SIDE, size_x), jnp.float32)] * 6,
+        compiler_params=pltpu.CompilerParams(vmem_limit_bytes=56 << 20),
+        cost_estimate=pl.CostEstimate(flops=200000000, bytes_accessed=8000000, transcendentals=0),
+    )(place, jnp.reshape(peak, (1,)), *velocity, *phi)
 
 
 def per_device(displacement, material, level_set):
-    energy, own_peak = slab_energy(displacement, material)
+    own_z, own_y, size_x = level_set.shape
+    low = shift_from(level_set, "wide", 0, MARGIN, True)
+    high = shift_from(level_set, "wide", 0, MARGIN, False)
+    phi = rows_beside(jnp.concatenate([low, level_set, high], axis=0), MARGIN)
+    energy, own_peak, phi = slab_energy(displacement, material, phi)
     devices = lax.axis_size("wide") * lax.axis_size("narrow")
     peaks = lax.all_to_all(
         jnp.full((devices, 1, 128), own_peak), ("wide", "narrow"), split_axis=0, concat_axis=0, tiled=True
     )
+    flipped = jnp.pad(jnp.transpose(energy, (2, 1, 0)), ((MARGIN, MARGIN), (0, 0), (0, 0)))
+    chunks = [
+        lax.slice_in_dim(flipped, k * own_z, k * own_z + own_z + 2 * MARGIN, axis=0)
+        for k in range(lax.axis_size("wide"))
+    ]
     moved = lax.all_to_all(
-        jnp.transpose(energy, (2, 1, 0)), "wide", split_axis=0, concat_axis=2, tiled=True
-    )
-    velocity = moved / (jnp.max(peaks) + 1e-06) - 0.5
-    vel_wide, phi_wide = (
-        with_halo(velocity, (("wide", 0), ("narrow", 1)), EXT_PASSES),
-        with_halo(level_set, (("wide", 0), ("narrow", 1)), EXT_PASSES),
-    )
-    weight_wide = 1.0 / (1.0 + 4.0 * phi_wide * phi_wide)
-    speed = vel_wide
-    for step in range(EXT_PASSES):
-        speed = ghost_fill(speed, EXT_PASSES - step, 0.0)
-        weight_in = inner_region(weight_wide, step + 1)
-        speed = weight_in * inner_region(vel_wide, step + 1) + (1.0 - weight_in) * neighbour_mean(
-            speed
-        )
-    phi = level_set
-    for step in range(HJ_STEPS):
-        beside_all = with_halo(phi, (("wide", 0), ("narrow", 1)), 3)
-        phi = march_step(ghost_fill(beside_all, 3, 1.0), speed)
-    return (phi, speed)
+        jnp.concatenate(chunks, axis=0), "wide", split_axis=0, concat_axis=2, tiled=True
+    )
+    return march(rows_beside(moved, MARGIN), phi, jnp.max(peaks), own_z, own_y)
 
 
 def solution(mesh):

time: 275 us -> 263 us (0.956)
  Pallas kernels: 36.6 us -> 113 us
  other arithmetic: 60.2 us -> 5.92 us
  starting transfers between devices: 79 us -> 32.7 us
  blocking collectives: 0 us -> 32.1 us
  waiting for transfers between devices: 58 us -> 31.4 us
  local copies, waits for them, and re-layouts: 37.9 us -> 45.8 us
    pallas_call x0 -> x1, Pallas kernels: none -> 76.2 us  [march(): pl.pallas_call(march_kernel, out_shape=(result, result), in_specs=[smem,...]
    ppermute x20 -> x0, starting transfers between devices: 53.8 us -> none  [the longest x10 36.8 us: with_halo(): lax.ppermute(lax.slice_in_dim(block, block.shape[dim] - width, None, axis...]
    sub x13 -> x0, other arithmetic: 43.1 us -> none  [the longest x3 37.7 us: march_step(): centre - TIME_STEP * (jnp.maximum(speed, 0.0) * jnp.sqrt(grow_plus) + jnp...]
    all_to_all x0 -> x1, blocking collectives: none -> 32.1 us  [per_device(): lax.all_to_all(jnp.concatenate(chunks, axis=0), 'wide', split_axis=0, con...]
    ppermute x20 -> x0, waiting for transfers between devices: 17.9 us -> none  [the longest x10 17.8 us: with_halo(): lax.ppermute(lax.slice_in_dim(block, 0, width, axis=dim), axis, backward)]
    ppermute x4 -> x10, starting transfers between devices: 12.5 us -> 29.4 us  [shift_from(): return lax.ppermute(part, axis, pairs)]
    select_n x5 -> x0, other arithmetic: 6.84 us -> none  [ghost_fill(): return jnp.where(inside, array, value)]
    all_to_all x1 -> x0, waiting for transfers between devices: 6.25 us -> none  [per_device(): lax.all_to_all(jnp.transpose(energy, (2, 1, 0)), 'wide', split_axis=0, co...]
  transfers between devices with their start and end apart: 26 -> 11, of which waited for: 9 -> 4; matrix products, arithmetic and copies ran while one was open for 16% -> 8% of each run, Pallas kernels for 13% -> 0%
where the time goes in v2:
time: 263 us; the launch traced here: 262 us
  Pallas kernels  113 us (43%)
  local copies, waits for them, and re-layouts  45.8 us (17%)
  starting transfers between devices  32.7 us (12%)
  blocking collectives  32.1 us (12%)
  waiting for transfers between devices  31.4 us (12%)
  other arithmetic  5.92 us (2%)
    pallas_call x1, Pallas kernels, march(): pl.pallas_call(march_kernel, out_shape=(result, result), in_specs=[smem,...  76.2 us
    pallas_call x1, Pallas kernels, slab_energy(): pl.pallas_call(energy_kernel, grid=(loads,), out_shape=(jax.ShapeDtypeStr...  36.6 us
    all_to_all x1, blocking collectives, per_device(): lax.all_to_all(jnp.concatenate(chunks, axis=0), 'wide', split_axis=0, con...  32.1 us
    ppermute x10, starting transfers between devices, shift_from(): return lax.ppermute(part, axis, pairs)  29.4 us
    ppermute x10, waiting for transfers between devices, shift_from(): return lax.ppermute(part, axis, pairs)  28.1 us
    unnamed x25, local copies, waits for them, and re-layouts  12.5 us
    all_to_all x3, local copies, waits for them, and re-layouts, per_device(): lax.all_to_all(jnp.concatenate(chunks, axis=0), 'wide', split_axis=0, con...  6.7 us
    slice x7, local copies, waits for them, and re-layouts, shift_from(): part = lax.slice_in_dim(block, 0, width, axis=dim)  5.81 us
  transfers between devices with their start and end apart: 11, of which 4 were waited for; matrix products, arithmetic and copies ran while one was open for 8% of the time, Pallas kernels for 0%

profile of v2, /device:TPU:1, one launch (start us, length us, event | category | flops | bytes accessed | tf_op | source)
XLA Modules:
  0.0 261.9 jit_solution(16829662235163998107)
XLA Ops:
  2.2 1.9 collective-permute-start
  5.8 4.5 %collective-permute-start.1 = (f32[3,3,16,1,384]{4,3,2,1,0:T(1,128)S(1)}, f32[3,3,16,1,384]{4,3,2,1,0:T(1,128)S(1)}, u32[]{:S(2)}, u32[]{:S(2)}) collective-permute-start(f32[3,3,16,1,384]{4,3,2,1,0:T(1,128)S(1)} %slice.81), channel_id=1, source_target_pairs={{0,1},{1,2},{2,3},{4,5},{5,6},{6,7},{8,9},{9,10},{10,11},{12,13},{... | collective-permute-start | bytes 663560 | tf_op jit(solution)/shard_map/ppermute | solution.py:31
  10.4 2.8 %collective-permute-done.1 = f32[3,3,16,1,384]{4,3,2,1,0:T(1,128)S(1)} collective-permute-done((f32[3,3,16,1,384]{4,3,2,1,0:T(1,128)S(1)}, f32[3,3,16,1,384]{4,3,2,1,0:T(1,128)S(1)}, u32[]{:S(2)}, u32[]{:S(2)}) %collective-permute-start.1) | collective-permute-done | bytes 221216 | tf_op jit(solution)/shard_map/ppermute | solution.py:31
  18.5 4.7 %collective-permute-start.4 = (f32[10,32,128]{2,1,0:T(8,128)S(1)}, f32[10,32,128]{2,1,0:T(8,128)}, u32[]{:S(2)}, u32[]{:S(2)}) collective-permute-start(f32[10,32,128]{2,1,0:T(8,128)S(1)} %get-tuple-element.29), channel_id=1, source_target_pairs={{0,4},{4,8},{8,12},{12,16},{16,20},{20,24},{24,28},{1,5},{5,9},{9,... | collective-permute-start | bytes 491528 | tf_op jit(solution)/shard_map/ppermute | solution.py:31
  26.4 2.3 copy.38.stiff_ref
  28.7 21.1 %collective-permute-done.4 = f32[10,32,128]{2,1,0:T(8,128)} collective-permute-done((f32[10,32,128]{2,1,0:T(8,128)S(1)}, f32[10,32,128]{2,1,0:T(8,128)}, u32[]{:S(2)}, u32[]{:S(2)}) %collective-permute-start.4) | collective-permute-done | bytes 163872 | tf_op jit(solution)/shard_map/ppermute | solution.py:31
  51.8 4.1 %collective-permute-start.3 = (f32[3,3,1,40,384]{4,3,2,1,0:T(8,128)S(1)}, f32[3,3,1,40,384]{4,3,2,1,0:T(8,128)S(1)}, u32[]{:S(2)}, u32[]{:S(2)}) collective-permute-start(f32[3,3,1,40,384]{4,3,2,1,0:T(8,128)S(1)} %slice.103), channel_id=1, source_target_pairs={{0,4},{4,8},{8,12},{12,16},{16,20},{20,24},{24,28},{1,5},{5,9},{9,... | collective-permute-start | bytes 1658888 | tf_op jit(solution)/shard_map/ppermute | solution.py:31
  56.2 3.5 %collective-permute-start.6 = (f32[68,10,128]{2,0,1:T(8,128)S(1)}, f32[68,10,128]{2,0,1:T(8,128)S(1)}, u32[]{:S(2)}, u32[]{:S(2)}) collective-permute-start(f32[68,10,128]{2,0,1:T(8,128)S(1)} %copy.36), channel_id=1, source_target_pairs={{0,1},{1,2},{2,3},{4,5},{5,6},{6,7},{8,9},{9,10},{10,11},{12,13},{... | collective-permute-start | bytes 1044488 | tf_op jit(solution)/shard_map/ppermute | solution.py:31
  59.8 1.9 collective-permute-start.7
  63.1 4.2 %collective-permute-done.3 = f32[3,3,1,40,384]{4,3,2,1,0:T(8,128)S(1)} collective-permute-done((f32[3,3,1,40,384]{4,3,2,1,0:T(8,128)S(1)}, f32[3,3,1,40,384]{4,3,2,1,0:T(8,128)S(1)}, u32[]{:S(2)}, u32[]{:S(2)}) %collective-permute-start.3) | collective-permute-done | bytes 552992 | tf_op jit(solution)/shard_map/ppermute | solution.py:31
  69.3 36.6 %shard_map.50 = (f32[16,32,384]{2,1,0:T(8,128)S(1)}, f32[32,384]{1,0:T(8,128)S(1)}) custom-call(f32[3,3,16,32,384]{4,3,2,1,0:T(8,128)S(1)} %bitcast.13, f32[3,3,3,32,384]{4,3,2,1,0:T(8,128)S(1)} %slice.104.xh_ref, f32[3,3,19,8,384]{4,3,2,1,0:T(8,128)S(1)} %pad_maximum_fusion.yh_ref, f32[16,32,384]{2,1,0:T(8,128)S(1)} %copy.38.stiff_ref), custom_call_target="tpu_custom_call" | custom-call | flops 100000000 | bytes 12000000 | tf_op jit(solution)/shard_map/pallas_call | solution.py:153
  107.5 2.9 %copy.40 = f32[544,32,16]{1,2,0:T(8,128)} copy(f32[544,32,16]{0,1,2:T(8,128)S(1)} %concatenate.31) | data formatting | bytes 2228224 | tf_op jit(solution)/shard_map/concatenate | solution.py:374
  110.4 4.1 %reshape.13 = f32[8,1,34816]{2,1,0:T(1,128)S(1)} reshape(f32[544,16,32]{2,1,0:T(8,128)} %bitcast.15) | data formatting | bytes 2228224
  114.5 32.1 %all_to_all.23 = f32[8,1,34816]{2,1,0:T(1,128)S(1)} all-to-all(f32[8,1,34816]{2,1,0:T(1,128)S(1)} %reshape.13), channel_id=1, replica_groups=mesh['wide'=8,'narrow'=4] {'wide'}, dimensions={0} | all-to-all | bytes 2228224 | tf_op jit(solution)/shard_map/all_to_all | solution.py:373
  147.1 3.3 %reduce = f32[8,34816]{1,0:T(8,128)S(1)} reduce(f32[8,1,34816]{2,1,0:T(1,128)S(1)} %all_to_all.23, f32[]{:T(128)} %broadcast.37), dimensions={1}, to_apply=%all_to_all.17.reduce_sub_computation | reduce | bytes 2228228 | tf_op jit(solution)/shard_map/all_to_all | solution.py:373
  150.4 3.5 %reshape.14 = f32[544,16,32]{2,1,0:T(8,128)} reshape(f32[8,34816]{1,0:T(8,128)S(1)} %reduce) | data formatting | bytes 2228224
  154.0 4.5 %copy.41 = f32[8,68,32,16]{1,3,0,2:T(8,128)S(1)} copy(f32[8,68,32,16]{2,3,1,0:T(8,128)} %bitcast.16) | data formatting | bytes 2228224 | tf_op jit(solution)/shard_map/all_to_all | solution.py:373
  159.4 2.1 copy.42
  161.5 4.3 %collective-permute-start.8 = (f32[68,10,128]{2,0,1:T(8,128)}, f32[68,10,128]{2,0,1:T(8,128)}, u32[]{:S(2)}, u32[]{:S(2)}) collective-permute-start(f32[68,10,128]{2,0,1:T(8,128)} %copy.42), channel_id=1, source_target_pairs={{0,1},{1,2},{2,3},{4,5},{5,6},{6,7},{8,9},{9,10},{10,11},{12,13},{... | collective-permute-start | bytes 1044488 | tf_op jit(solution)/shard_map/ppermute | solution.py:31
  166.8 1.9 collective-permute-start.9
  170.5 3.3 %all-to-all-start = ((f32[32,1,128]{2,1,0:T(1,128)}), f32[32,1,128]{2,1,0:T(1,128)S(1)}, u32[]{:S(2)}, u32[]{:S(2)}) async-start(f32[32,1,128]{2,1,0:T(1,128)} %broadcast_in_dim.11), calls=%async_computation | async-start | bytes 32768 | tf_op jit(solution)/shard_map/all_to_all | solution.py:365
  175.4 1.9 copy.48.phi_high
  177.3 3.3 %all-to-all-done = f32[32,1,128]{2,1,0:T(1,128)S(1)} async-done(((f32[32,1,128]{2,1,0:T(1,128)}), f32[32,1,128]{2,1,0:T(1,128)S(1)}, u32[]{:S(2)}, u32[]{:S(2)}) %all-to-all-start) | async-done | bytes 16416 | tf_op jit(solution)/shard_map/all_to_all | solution.py:365
  185.7 76.2 %shard_map.51 = (f32[48,32,128]{2,1,0:T(8,128)}, f32[48,32,128]{2,1,0:T(8,128)}) custom-call(s32[4]{0:T(128)} %pad_add_fusion.place, f32[1]{0:T(128)} %bitcast.4.peak, f32[68,32,128]{2,1,0:T(8,128)} %copy.44.vel_own, f32[68,10,128]{2,1,0:T(8,128)} %copy.45.vel_low, f32[68,10,128]{2,1,0:T(8,128)} %copy.46.vel_high, f32[68,32,128]{2,1,0:T(8,128)} %copy-done.1, ...), custom_call_target="tpu_custom_call" | custom-call | flops 200000000 | bytes 8000000 | tf_op jit(solution)/shard_map/pallas_call | solution.py:347
  (67 shorter events, 29.8 us)
Async XLA Ops:
  2.2 11.0 %collective-permute-start = (f32[3,3,16,2,384]{4,3,2,1,0:T(2,128)S(1)}, f32[3,3,16,2,384]{4,3,2,1,0:T(2,128)S(1)}, u32[]{:S(2)}, u32[]{:S(2)}) collective-permute-start(f32[3,3,16,2,384]{4,3,2,1,0:T(2,128)S(1)} %slice.80), channel_id=1, source_target_pairs={{1,0},{2,1},{3,2},{5,4},{6,5},{7,6},{9,8},{10,9},{11,10},{13,12},{... | collective-permute-start | bytes 1327112 | tf_op jit(solution)/shard_map/ppermute | solution.py:31
  5.8 7.4 %collective-permute-start.1 = (f32[3,3,16,1,384]{4,3,2,1,0:T(1,128)S(1)}, f32[3,3,16,1,384]{4,3,2,1,0:T(1,128)S(1)}, u32[]{:S(2)}, u32[]{:S(2)}) collective-permute-start(f32[3,3,16,1,384]{4,3,2,1,0:T(1,128)S(1)} %slice.81), channel_id=1, source_target_pairs={{0,1},{1,2},{2,3},{4,5},{5,6},{6,7},{8,9},{9,10},{10,11},{12,13},{... | collective-permute-start | bytes 663560 | tf_op jit(solution)/shard_map/ppermute | solution.py:31
  10.4 3.0 %slice-start.2 = ((f32[3,3,16,32,384]{4,3,2,1,0:T(8,128)}), f32[3,3,2,32,384]{4,3,2,1,0:T(8,128)S(1)}, s32[]{:S(2)}) async-start(f32[3,3,16,32,384]{4,3,2,1,0:T(8,128)} %own_ref.1), calls=%async_computation.4 | async-start | bytes 1769472 | tf_op jit(solution)/shard_map/slice | solution.py:139
  10.4 3.0 %slice-start.3 = ((f32[3,3,16,32,384]{4,3,2,1,0:T(8,128)}), f32[3,3,1,32,384]{4,3,2,1,0:T(8,128)S(1)}, s32[]{:S(2)}) async-start(f32[3,3,16,32,384]{4,3,2,1,0:T(8,128)} %own_ref.1), calls=%async_computation.5 | async-start | bytes 884736 | tf_op jit(solution)/shard_map/slice | solution.py:139
  13.2 0.7 copy-start.3
  13.9 1.2 copy-start
  15.1 9.3 %copy-start.7 = (s32[16,32,24]{1,2,0:T(8,128)S(1)}, s32[16,32,24]{1,2,0:T(8,128)}, u32[]{:S(2)}) copy-start(s32[16,32,24]{1,2,0:T(8,128)} %param.4) | copy-start | bytes 147460
  16.2 45.6 %collective-permute-start.2 = (f32[3,3,2,40,384]{4,3,2,1,0:T(8,128)}, f32[3,3,2,40,384]{4,3,2,1,0:T(8,128)}, u32[]{:S(2)}, u32[]{:S(2)}) collective-permute-start(f32[3,3,2,40,384]{4,3,2,1,0:T(8,128)} %slice.102), channel_id=1, source_target_pairs={{4,0},{8,4},{12,8},{16,12},{20,16},{24,20},{28,24},{5,1},{9,5},{13... | collective-permute-start | bytes 3317768 | tf_op jit(solution)/shard_map/ppermute | solution.py:31
  18.5 31.3 %collective-permute-start.4 = (f32[10,32,128]{2,1,0:T(8,128)S(1)}, f32[10,32,128]{2,1,0:T(8,128)}, u32[]{:S(2)}, u32[]{:S(2)}) collective-permute-start(f32[10,32,128]{2,1,0:T(8,128)S(1)} %get-tuple-element.29), channel_id=1, source_target_pairs={{0,4},{4,8},{8,12},{12,16},{16,20},{20,24},{24,28},{1,5},{5,9},{9,... | collective-permute-start | bytes 491528 | tf_op jit(solution)/shard_map/ppermute | solution.py:31
  23.2 32.8 %collective-permute-start.5 = (f32[10,32,128]{2,1,0:T(8,128)S(1)}, f32[10,32,128]{2,1,0:T(8,128)S(1)}, u32[]{:S(2)}, u32[]{:S(2)}) collective-permute-start(f32[10,32,128]{2,1,0:T(8,128)S(1)} %get-tuple-element.28), channel_id=1, source_target_pairs={{4,0},{8,4},{12,8},{16,12},{20,16},{24,20},{28,24},{5,1},{9,5},{13... | collective-permute-start | bytes 491528 | tf_op jit(solution)/shard_map/ppermute | solution.py:31
  28.7 27.2 %copy-start.2 = (f32[48,32,128]{2,1,0:T(8,128)S(1)}, f32[48,32,128]{2,1,0:T(8,128)}, u32[]{:S(2)}) copy-start(f32[48,32,128]{2,1,0:T(8,128)} %param.5) | copy-start | bytes 2359300
  51.8 15.5 %collective-permute-start.3 = (f32[3,3,1,40,384]{4,3,2,1,0:T(8,128)S(1)}, f32[3,3,1,40,384]{4,3,2,1,0:T(8,128)S(1)}, u32[]{:S(2)}, u32[]{:S(2)}) collective-permute-start(f32[3,3,1,40,384]{4,3,2,1,0:T(8,128)S(1)} %slice.103), channel_id=1, source_target_pairs={{0,4},{4,8},{8,12},{12,16},{16,20},{20,24},{24,28},{1,5},{5,9},{9,... | collective-permute-start | bytes 1658888 | tf_op jit(solution)/shard_map/ppermute | solution.py:31
  56.0 3.9 %copy-start.1 = (f32[68,32,128]{2,1,0:T(8,128)}, f32[68,32,128]{2,1,0:T(8,128)S(1)}, u32[]{:S(2)}) copy-start(f32[68,32,128]{2,1,0:T(8,128)S(1)} %constant_dynamic-update-slice_fusion.2.phi_own) | copy-start | bytes 3342340
  56.0 12.9 %slice-start = ((s8[7077888]{0:T(1024)(128)(4,1)}), s8[4194304]{0:T(1024)(128)(4,1)S(1)}, s32[]{:S(2)}) async-start(s8[7077888]{0:T(1024)(128)(4,1)} %bitcast.12), calls=%async_computation.2 | async-start | bytes 8388608
  56.2 12.7 %collective-permute-start.6 = (f32[68,10,128]{2,0,1:T(8,128)S(1)}, f32[68,10,128]{2,0,1:T(8,128)S(1)}, u32[]{:S(2)}, u32[]{:S(2)}) collective-permute-start(f32[68,10,128]{2,0,1:T(8,128)S(1)} %copy.36), channel_id=1, source_target_pairs={{0,1},{1,2},{2,3},{4,5},{5,6},{6,7},{8,9},{9,10},{10,11},{12,13},{... | collective-permute-start | bytes 1044488 | tf_op jit(solution)/shard_map/ppermute | solution.py:31
  59.8 9.1 %collective-permute-start.7 = (f32[68,10,128]{2,0,1:T(8,128)S(1)}, f32[68,10,128]{2,0,1:T(8,128)}, u32[]{:S(2)}, u32[]{:S(2)}) collective-permute-start(f32[68,10,128]{2,0,1:T(8,128)S(1)} %copy.37), channel_id=1, source_target_pairs={{1,0},{2,1},{3,2},{5,4},{6,5},{7,6},{9,8},{10,9},{11,10},{13,12},{... | collective-permute-start | bytes 1044488 | tf_op jit(solution)/shard_map/ppermute | solution.py:31
  67.4 0.9 copy-start.4
  67.4 1.9 slice-start.1
  68.9 37.0 %copy-start.5 = (f32[68,10,128]{2,0,1:T(8,128)}, f32[68,10,128]{2,0,1:T(8,128)S(1)}, u32[]{:S(2)}) copy-start(f32[68,10,128]{2,0,1:T(8,128)S(1)} %collective-permute-done.6) | copy-start | bytes 1044484
  159.4 15.1 %copy-start.6 = (f32[68,10,128]{2,0,1:T(8,128)S(1)}, f32[68,10,128]{2,0,1:T(8,128)}, u32[]{:S(2)}) copy-start(f32[68,10,128]{2,0,1:T(8,128)} %copy-done.5) | copy-start | bytes 1044484
  161.5 21.4 %collective-permute-start.8 = (f32[68,10,128]{2,0,1:T(8,128)}, f32[68,10,128]{2,0,1:T(8,128)}, u32[]{:S(2)}, u32[]{:S(2)}) collective-permute-start(f32[68,10,128]{2,0,1:T(8,128)} %copy.42), channel_id=1, source_target_pairs={{0,1},{1,2},{2,3},{4,5},{5,6},{6,7},{8,9},{9,10},{10,11},{12,13},{... | collective-permute-start | bytes 1044488 | tf_op jit(solution)/shard_map/ppermute | solution.py:31
  166.8 18.0 %collective-permute-start.9 = (f32[68,10,128]{2,0,1:T(8,128)}, f32[68,10,128]{2,0,1:T(8,128)S(1)}, u32[]{:S(2)}, u32[]{:S(2)}) collective-permute-start(f32[68,10,128]{2,0,1:T(8,128)} %copy.43), channel_id=1, source_target_pairs={{1,0},{2,1},{3,2},{5,4},{6,5},{7,6},{9,8},{10,9},{11,10},{13,12},{... | collective-permute-start | bytes 1044488 | tf_op jit(solution)/shard_map/ppermute | solution.py:31
  170.5 10.1 %all-to-all-start = ((f32[32,1,128]{2,1,0:T(1,128)}), f32[32,1,128]{2,1,0:T(1,128)S(1)}, u32[]{:S(2)}, u32[]{:S(2)}) async-start(f32[32,1,128]{2,1,0:T(1,128)} %broadcast_in_dim.11), calls=%async_computation | async-start | bytes 32768 | tf_op jit(solution)/shard_map/all_to_all | solution.py:365

commit v3 on v2

--- a/solution.py
+++ b/solution.py
@@ -43,9 +43,10 @@
     return val, der
 
 
-def energy_kernel(own_ref, xh_ref, yh_ref, stiff_ref, out_ref, peak_ref, val_ref, der_ref):
+def energy_kernel(jump, own_ref, yh_ref, stiff_ref, out_ref, peak_ref, val_ref, der_ref):
     load = pl.program_id(0)
-    size_x, size_y, size_z = own_ref.shape[2:]
+    planes, size_y, size_z = own_ref.shape[2:]
+    made = out_ref.shape[0]
     rows = val_ref.shape[2]
 
     def plane(c, p, body, tail):
@@ -57,13 +58,9 @@
         der_ref[c, p, size_y:rows, :] = der
 
     for c in range(3):
-        @pl.loop(0, size_x)
+        @pl.loop(0, planes)
         def _(p):
             plane(c, p, own_ref[0, c, p], yh_ref[0, c, p])
-
-        @pl.loop(0, 3)
-        def _(q):
-            plane(c, size_x + q, xh_ref[0, c, q], yh_ref[0, c, size_x + q])
 
     def taps_x(ref, c, idx, cols):
         parts = [ref[c, i, :, cols] for i in idx]
@@ -85,10 +82,10 @@
 
     chunk = 128
 
-    @pl.loop(0, size_x)
+    @pl.loop(0, made)
     def _(p):
-        low = jnp.where(p == 0, size_x + 2, p - 1)
-        idx = (low, p, p + 1, p + 2)
+        base = jnp.where(p == 0, 0, p + jump) if jump else p
+        idx = (base, base + 1, base + 2, base + 3)
         for piece in range(size_z // chunk):
             cols = pl.ds(piece * chunk, chunk)
             fields = []
@@ -121,60 +118,64 @@
     def _():
         peak_ref[...] = jnp.zeros(peak_ref.shape, jnp.float32)
 
-        @pl.loop(0, size_x)
+        @pl.loop(0, made)
         def _(p):
             energy = stiff_ref[p] * out_ref[p]
             out_ref[p] = energy
             peak_ref[...] = jnp.maximum(peak_ref[...], energy)
 
 
+def energy_of(planes, tail, stiffness, jump):
+    loads, comps, count, size_y, size_z = planes.shape
+    made = stiffness.shape[0]
+    return pl.pallas_call(
+        functools.partial(energy_kernel, jump),
+        grid=(loads,),
+        out_shape=(
+            jax.ShapeDtypeStruct((made, size_y, size_z), jnp.float32),
+            jax.ShapeDtypeStruct((size_y, size_z), jnp.float32),
+        ),
+        in_specs=[
+            pl.BlockSpec((1, comps, count, size_y, size_z), lambda i: (i, 0, 0, 0, 0)),
+            pl.BlockSpec((1, comps, count, 8, size_z), lambda i: (i, 0, 0, 0, 0)),
+            pl.BlockSpec((made, size_y, size_z), lambda i: (0, 0, 0)),
+        ],
+        out_specs=(
+            pl.BlockSpec((made, size_y, size_z), lambda i: (0, 0, 0)),
+            pl.BlockSpec((size_y, size_z), lambda i: (0, 0)),
+        ),
+        scratch_shapes=[pltpu.VMEM((comps, count, size_y + 8, size_z), jnp.float32)] * 2,
+        compiler_params=pltpu.CompilerParams(vmem_limit_bytes=40 << 20),
+        cost_estimate=pl.CostEstimate(
+            flops=6000000 * made, bytes_accessed=6000000 * made, transcendentals=0
+        ),
+    )(planes, tail, stiffness)
+
+
 def slab_energy(displacement, material, early):
     loads, comps, size_x, size_y, size_z = displacement.shape
+    high_x = shift_from(displacement, "wide", 2, 2, False)
+    low_x = shift_from(displacement, "wide", 2, 1, True)
     low_y = shift_from(displacement, "narrow", 3, 1, True)
     high_y = shift_from(displacement, "narrow", 3, 2, False)
     filler = jnp.zeros((loads, comps, size_x, 5, size_z), jnp.float32)
     tail = jnp.concatenate([high_y, filler, low_y], axis=3)
-    ends = jnp.concatenate(
-        [
-            jnp.concatenate([displacement[:, :, :2], displacement[:, :, -1:]], axis=2),
-            jnp.concatenate([tail[:, :, :2], tail[:, :, -1:]], axis=2),
-        ],
-        axis=3,
-    )
-    high_x = shift_from(ends, "wide", 2, 2, False)
-    low_x = shift_from(ends, "wide", 2, 1, True)
-    beside = jnp.concatenate([high_x, low_x], axis=2)
-    beside_own = beside[:, :, :, :size_y]
-    tail = jnp.concatenate([tail, beside[:, :, :, size_y:]], axis=2)
+    high_tail = shift_from(tail, "wide", 2, 2, False)
+    low_tail = shift_from(tail, "wide", 2, 1, True)
     stiffness = 0.2 + 0.8 * jnp.repeat(material.astype(jnp.float32), BZ, axis=2)
-    beside_own, tail, early = lax.optimization_barrier((beside_own, tail, early))
-    planes = size_x + 3
-    rows = size_y + 8
-    energy, peak = pl.pallas_call(
-        energy_kernel,
-        grid=(loads,),
-        out_shape=(
-            jax.ShapeDtypeStruct((size_x, size_y, size_z), jnp.float32),
-            jax.ShapeDtypeStruct((size_y, size_z), jnp.float32),
-        ),
-        in_specs=[
-            pl.BlockSpec((1, comps, size_x, size_y, size_z), lambda i: (i, 0, 0, 0, 0)),
-            pl.BlockSpec((1, comps, 3, size_y, size_z), lambda i: (i, 0, 0, 0, 0)),
-            pl.BlockSpec((1, comps, planes, 8, size_z), lambda i: (i, 0, 0, 0, 0)),
-            pl.BlockSpec((size_x, size_y, size_z), lambda i: (0, 0, 0)),
-        ],
-        out_specs=(
-            pl.BlockSpec((size_x, size_y, size_z), lambda i: (0, 0, 0)),
-            pl.BlockSpec((size_y, size_z), lambda i: (0, 0)),
-        ),
-        scratch_shapes=[
-            pltpu.VMEM((comps, planes, rows, size_z), jnp.float32),
-            pltpu.VMEM((comps, planes, rows, size_z), jnp.float32),
-        ],
-        compiler_params=pltpu.CompilerParams(vmem_limit_bytes=40 << 20),
-        cost_estimate=pl.CostEstimate(flops=100000000, bytes_accessed=12000000, transcendentals=0),
-    )(displacement, beside_own, tail, stiffness)
-    return energy, jnp.max(peak), early
+    inner, inner_peak = energy_of(displacement, tail, stiffness[1 : size_x - 2], 0)
+
+    def edges(block, low, high):
+        return jnp.concatenate([low, block[:, :, :3], block[:, :, size_x - 3 :], high], axis=2)
+
+    beside, beside_tail, early = lax.optimization_barrier(
+        (edges(displacement, low_x, high_x), edges(tail, low_tail, high_tail), early)
+    )
+    rim, rim_peak = energy_of(
+        beside, beside_tail, jnp.concatenate([stiffness[:1], stiffness[size_x - 2 :]], axis=0), 3
+    )
+    energy = jnp.concatenate([rim[:1], inner, rim[1:]], axis=0)
+    return energy, jnp.max(jnp.maximum(inner_peak, rim_peak)), early
 
 
 def weno_pair(d):

time: 263 us -> 275 us (1.046)
  waiting for transfers between devices: 31.4 us -> 20 us
  local copies, waits for them, and re-layouts: 45.8 us -> 54.6 us
  Pallas kernels: 113 us -> 120 us
  starting transfers between devices: 32.7 us -> 39.3 us
  other arithmetic: 5.92 us -> 9.38 us
  blocking collectives: 32.1 us -> 29.1 us
    ppermute x10 -> x12, waiting for transfers between devices: 28.1 us -> 17.6 us  [shift_from(): return lax.ppermute(part, axis, pairs)]
    slice x6 -> x11, local copies, waits for them, and re-layouts: 0.19 us -> 10.1 us  [the longest x2 3.53 us: edges(): block[:, :, :3]]
    pallas_call x1 -> x2, Pallas kernels: 36.6 us -> 43.4 us  [energy_of(): pl.pallas_call(functools.partial(energy_kernel, jump), grid=(loads,), out...]
    ppermute x10 -> x12, starting transfers between devices: 29.4 us -> 35.9 us  [shift_from(): return lax.ppermute(part, axis, pairs)]
    concatenate x2 -> x4, other arithmetic: 0.76 us -> 4.14 us  [the longest x2 1.71 us: edges(): jnp.concatenate([low, block[:, :, :3], block[:, :, size_x - 3:], high], a...]
    all_to_all x1, blocking collectives: 32.1 us -> 29.1 us  [per_device(): lax.all_to_all(jnp.concatenate(chunks, axis=0), 'wide', split_axis=0, con...]
    unnamed x25 -> x24, local copies, waits for them, and re-layouts: 12.5 us -> 9.73 us
    slice x7 -> x8, local copies, waits for them, and re-layouts: 5.81 us -> 7.57 us  [shift_from(): part = lax.slice_in_dim(block, 0, width, axis=dim)]
  transfers between devices with their start and end apart: 11 -> 13, of which waited for: 4 -> 4; matrix products, arithmetic and copies ran while one was open for 8% -> 14% of each run, Pallas kernels for 0% -> 11%
where the time goes in v3:
time: 275 us; the launch traced here: 273 us
  Pallas kernels  120 us (44%)
  local copies, waits for them, and re-layouts  54.6 us (20%)
  starting transfers between devices  39.3 us (14%)
  blocking collectives  29.1 us (11%)
  waiting for transfers between devices  20 us (7%)
  other arithmetic  9.38 us (3%)
    pallas_call x1, Pallas kernels, march(): pl.pallas_call(march_kernel, out_shape=(result, result), in_specs=[smem,...  76.3 us
    pallas_call x2, Pallas kernels, energy_of(): pl.pallas_call(functools.partial(energy_kernel, jump), grid=(loads,), out...  43.4 us
    ppermute x12, starting transfers between devices, shift_from(): return lax.ppermute(part, axis, pairs)  35.9 us
    all_to_all x1, blocking collectives, per_device(): lax.all_to_all(jnp.concatenate(chunks, axis=0), 'wide', split_axis=0, con...  29.1 us
    ppermute x12, waiting for transfers between devices, shift_from(): return lax.ppermute(part, axis, pairs)  17.6 us
    unnamed x24, local copies, waits for them, and re-layouts  9.73 us
    slice x8, local copies, waits for them, and re-layouts, shift_from(): part = lax.slice_in_dim(block, 0, width, axis=dim)  7.57 us
    all_to_all x3, local copies, waits for them, and re-layouts, per_device(): lax.all_to_all(jnp.concatenate(chunks, axis=0), 'wide', split_axis=0, con...  6.71 us
  transfers between devices with their start and end apart: 13, of which 4 were waited for; matrix products, arithmetic and copies ran while one was open for 14% of the time, Pallas kernels for 11%

profile of v3, /device:TPU:1, one launch (start us, length us, event | category | flops | bytes accessed | tf_op | source)
XLA Modules:
  0.0 273.1 jit_solution(7343935999603244166)
XLA Ops:
  0.6 2.4 slice.108
  3.0 4.5 %collective-permute-start.1 = (f32[3,3,16,1,384]{4,3,2,1,0:T(1,128)}, f32[3,3,16,1,384]{4,3,2,1,0:T(1,128)}, u32[]{:S(2)}, u32[]{:S(2)}) collective-permute-start(f32[3,3,16,1,384]{4,3,2,1,0:T(1,128)} %slice.108), channel_id=1, source_target_pairs={{0,1},{1,2},{2,3},{4,5},{5,6},{6,7},{8,9},{9,10},{10,11},{12,13},{... | collective-permute-start | bytes 663560 | tf_op jit(solution)/shard_map/ppermute | solution.py:31
  7.5 2.4 slice.107
  17.1 4.8 %collective-permute-start.2 = (f32[3,3,1,32,384]{4,3,2,1,0:T(8,128)}, f32[3,3,1,32,384]{4,3,2,1,0:T(8,128)}, u32[]{:S(2)}, u32[]{:S(2)}) collective-permute-start(f32[3,3,1,32,384]{4,3,2,1,0:T(8,128)} %slice.111), channel_id=1, source_target_pairs={{0,4},{4,8},{8,12},{12,16},{16,20},{20,24},{24,28},{1,5},{5,9},{9,... | collective-permute-start | bytes 1327112 | tf_op jit(solution)/shard_map/ppermute | solution.py:31
  23.6 4.0 %collective-permute-start.6 = (f32[10,32,128]{2,1,0:T(8,128)}, f32[10,32,128]{2,1,0:T(8,128)}, u32[]{:S(2)}, u32[]{:S(2)}) collective-permute-start(f32[10,32,128]{2,1,0:T(8,128)} %get-tuple-element.37), channel_id=1, source_target_pairs={{0,4},{4,8},{8,12},{12,16},{16,20},{20,24},{24,28},{1,5},{5,9},{9,... | collective-permute-start | bytes 491528 | tf_op jit(solution)/shard_map/ppermute | solution.py:31
  27.6 3.5 %fusion = (f32[3,3,3,32,384]{4,3,2,1,0:T(8,128)}, f32[3,3,3,32,384]{4,3,2,1,0:T(8,128)}) fusion(f32[3,3,16,32,384]{4,3,2,1,0:T(8,128)} %own_ref.1), kind=kLoop, calls=%fused_computation.14 | loop fusion | bytes 5308416 | tf_op jit(solution)/shard_map/slice | solution.py:169
  33.5 2.4 copy.44.stiff_ref
  42.6 7.4 %collective-permute-done.6 = f32[10,32,128]{2,1,0:T(8,128)} collective-permute-done((f32[10,32,128]{2,1,0:T(8,128)}, f32[10,32,128]{2,1,0:T(8,128)}, u32[]{:S(2)}, u32[]{:S(2)}) %collective-permute-start.6) | collective-permute-done | bytes 163872 | tf_op jit(solution)/shard_map/ppermute | solution.py:31
  53.4 5.0 %collective-permute-done.7 = f32[10,32,128]{2,1,0:T(8,128)S(1)} collective-permute-done((f32[10,32,128]{2,1,0:T(8,128)}, f32[10,32,128]{2,1,0:T(8,128)S(1)}, u32[]{:S(2)}, u32[]{:S(2)}) %collective-permute-start.7) | collective-permute-done | bytes 163872 | tf_op jit(solution)/shard_map/ppermute | solution.py:31
  58.6 4.7 %collective-permute-start.8 = (f32[68,10,128]{2,0,1:T(8,128)S(1)}, f32[68,10,128]{2,0,1:T(8,128)S(1)}, u32[]{:S(2)}, u32[]{:S(2)}) collective-permute-start(f32[68,10,128]{2,0,1:T(8,128)S(1)} %copy.45), channel_id=1, source_target_pairs={{0,1},{1,2},{2,3},{4,5},{5,6},{6,7},{8,9},{9,10},{10,11},{12,13},{... | collective-permute-start | bytes 1044488 | tf_op jit(solution)/shard_map/ppermute | solution.py:31
  66.4 4.9 %collective-permute-start.4 = (f32[3,3,1,8,384]{4,3,2,1,0:T(8,128)S(1)}, f32[3,3,1,8,384]{4,3,2,1,0:T(8,128)S(1)}, u32[]{:S(2)}, u32[]{:S(2)}) collective-permute-start(f32[3,3,1,8,384]{4,3,2,1,0:T(8,128)S(1)} %slice.141), channel_id=1, source_target_pairs={{0,4},{4,8},{8,12},{12,16},{16,20},{20,24},{24,28},{1,5},{5,9},{9,... | collective-permute-start | bytes 331784 | tf_op jit(solution)/shard_map/ppermute | solution.py:31
  71.4 30.4 %shard_map.50 = (f32[13,32,384]{2,1,0:T(8,128)S(1)}, f32[32,384]{1,0:T(8,128)S(1)}) custom-call(f32[3,3,16,32,384]{4,3,2,1,0:T(8,128)S(1)} %bitcast.18, f32[3,3,16,8,384]{4,3,2,1,0:T(8,128)S(1)} %pad_maximum_fusion.1.yh_ref, f32[13,32,384]{2,1,0:T(8,128)S(1)} %copy.44.stiff_ref), custom_call_target="tpu_custom_call" | custom-call | flops 78000000 | bytes 78000000 | tf_op jit(solution)/shard_map/pallas_call | solution.py:131
  105.7 5.2 %collective-permute-done.9 = f32[68,10,128]{2,0,1:T(8,128)} collective-permute-done((f32[68,10,128]{2,0,1:T(8,128)S(1)}, f32[68,10,128]{2,0,1:T(8,128)}, u32[]{:S(2)}, u32[]{:S(2)}) %collective-permute-start.9) | collective-permute-done | bytes 348192 | tf_op jit(solution)/shard_map/ppermute | solution.py:31
  110.9 13.0 %shard_map.51 = (f32[3,32,384]{2,1,0:T(8,128)S(1)}, f32[32,384]{1,0:T(8,128)S(1)}) custom-call(f32[3,3,9,32,384]{4,3,2,1,0:T(8,128)S(1)} %pad_maximum_fusion.own_ref, f32[3,3,9,8,384]{4,3,2,1,0:T(8,128)S(1)} %pad_maximum_fusion.2.yh_ref, f32[3,32,384]{2,1,0:T(8,128)S(1)} %pad_maximum_fusion.3.stiff_ref), custom_call_target="tpu_custom_call" | custom-call | flops 18000000 | bytes 18000000 | tf_op jit(solution)/shard_map/pallas_call | solution.py:131
  125.6 2.9 %copy.50 = f32[544,32,16]{1,2,0:T(8,128)} copy(f32[544,32,16]{0,1,2:T(8,128)S(1)} %concatenate.27) | data formatting | bytes 2228224 | tf_op jit(solution)/shard_map/concatenate | solution.py:375
  128.5 4.1 %reshape.17 = f32[8,1,34816]{2,1,0:T(1,128)S(1)} reshape(f32[544,16,32]{2,1,0:T(8,128)} %bitcast.19) | data formatting | bytes 2228224
  132.6 29.1 %all_to_all.23 = f32[8,1,34816]{2,1,0:T(1,128)S(1)} all-to-all(f32[8,1,34816]{2,1,0:T(1,128)S(1)} %reshape.17), channel_id=1, replica_groups=mesh['wide'=8,'narrow'=4] {'wide'}, dimensions={0} | all-to-all | bytes 2228224 | tf_op jit(solution)/shard_map/all_to_all | solution.py:374
  162.1 3.3 %reduce = f32[8,34816]{1,0:T(8,128)S(1)} reduce(f32[8,1,34816]{2,1,0:T(1,128)S(1)} %all_to_all.23, f32[]{:T(128)} %broadcast.16), dimensions={1}, to_apply=%all_to_all.17.reduce_sub_computation | reduce | bytes 2228228 | tf_op jit(solution)/shard_map/all_to_all | solution.py:374
  165.4 3.5 %reshape.18 = f32[544,16,32]{2,1,0:T(8,128)} reshape(f32[8,34816]{1,0:T(8,128)S(1)} %reduce) | data formatting | bytes 2228224
  169.0 4.5 %copy.51 = f32[8,68,32,16]{1,3,0,2:T(8,128)S(1)} copy(f32[8,68,32,16]{2,3,1,0:T(8,128)} %bitcast.20) | data formatting | bytes 2228224 | tf_op jit(solution)/shard_map/all_to_all | solution.py:374
  174.5 3.2 %collective-permute-start.10 = (f32[68,10,128]{2,0,1:T(8,128)}, f32[68,10,128]{2,0,1:T(8,128)S(1)}, u32[]{:S(2)}, u32[]{:S(2)}) collective-permute-start(f32[68,10,128]{2,0,1:T(8,128)} %copy.52), channel_id=1, source_target_pairs={{0,1},{1,2},{2,3},{4,5},{5,6},{6,7},{8,9},{9,10},{10,11},{12,13},{... | collective-permute-start | bytes 1044488 | tf_op jit(solution)/shard_map/ppermute | solution.py:31
  182.5 3.4 %all-to-all-start = ((f32[32,1,128]{2,1,0:T(1,128)}), f32[32,1,128]{2,1,0:T(1,128)S(1)}, u32[]{:S(2)}, u32[]{:S(2)}) async-start(f32[32,1,128]{2,1,0:T(1,128)} %broadcast_in_dim.17), calls=%async_computation | async-start | bytes 32768 | tf_op jit(solution)/shard_map/all_to_all | solution.py:366
  190.3 2.4 all-to-all-done
  196.8 76.3 %shard_map.52 = (f32[48,32,128]{2,1,0:T(8,128)}, f32[48,32,128]{2,1,0:T(8,128)}) custom-call(s32[4]{0:T(128)} %pad_add_fusion.place, f32[1]{0:T(128)} %bitcast.7.peak, f32[68,32,128]{2,1,0:T(8,128)} %copy.54.vel_own, f32[68,10,128]{2,1,0:T(8,128)} %copy.55.vel_low, f32[68,10,128]{2,1,0:T(8,128)} %copy.56.vel_high, f32[68,32,128]{2,1,0:T(8,128)} %copy-done.4, ...), custom_call_target="tpu_custom_call" | custom-call | flops 200000000 | bytes 8000000 | tf_op jit(solution)/shard_map/pallas_call | solution.py:348
  (82 shorter events, 44.8 us)
Async XLA Ops:
  3.0 60.5 %collective-permute-start.1 = (f32[3,3,16,1,384]{4,3,2,1,0:T(1,128)}, f32[3,3,16,1,384]{4,3,2,1,0:T(1,128)}, u32[]{:S(2)}, u32[]{:S(2)}) collective-permute-start(f32[3,3,16,1,384]{4,3,2,1,0:T(1,128)} %slice.108), channel_id=1, source_target_pairs={{0,1},{1,2},{2,3},{4,5},{5,6},{6,7},{8,9},{9,10},{10,11},{12,13},{... | collective-permute-start | bytes 663560 | tf_op jit(solution)/shard_map/ppermute | solution.py:31
  9.9 53.6 %collective-permute-start = (f32[3,3,16,2,384]{4,3,2,1,0:T(2,128)}, f32[3,3,16,2,384]{4,3,2,1,0:T(2,128)}, u32[]{:S(2)}, u32[]{:S(2)}) collective-permute-start(f32[3,3,16,2,384]{4,3,2,1,0:T(2,128)} %slice.107), channel_id=1, source_target_pairs={{1,0},{2,1},{3,2},{5,4},{6,5},{7,6},{9,8},{10,9},{11,10},{13,12},{... | collective-permute-start | bytes 1327112 | tf_op jit(solution)/shard_map/ppermute | solution.py:31
  14.0 90.0 %collective-permute-start.3 = (f32[3,3,2,32,384]{4,3,2,1,0:T(8,128)}, f32[3,3,2,32,384]{4,3,2,1,0:T(8,128)}, u32[]{:S(2)}, u32[]{:S(2)}) collective-permute-start(f32[3,3,2,32,384]{4,3,2,1,0:T(8,128)} %slice.114), channel_id=1, source_target_pairs={{4,0},{8,4},{12,8},{16,12},{20,16},{24,20},{28,24},{5,1},{9,5},{13... | collective-permute-start | bytes 2654216 | tf_op jit(solution)/shard_map/ppermute | solution.py:31
  17.1 86.9 %collective-permute-start.2 = (f32[3,3,1,32,384]{4,3,2,1,0:T(8,128)}, f32[3,3,1,32,384]{4,3,2,1,0:T(8,128)}, u32[]{:S(2)}, u32[]{:S(2)}) collective-permute-start(f32[3,3,1,32,384]{4,3,2,1,0:T(8,128)} %slice.111), channel_id=1, source_target_pairs={{0,4},{4,8},{8,12},{12,16},{16,20},{20,24},{24,28},{1,5},{5,9},{9,... | collective-permute-start | bytes 1327112 | tf_op jit(solution)/shard_map/ppermute | solution.py:31
  23.6 7.5 %copy-start.7 = (s32[16,32,24]{1,2,0:T(8,128)S(1)}, s32[16,32,24]{1,2,0:T(8,128)}, u32[]{:S(2)}) copy-start(s32[16,32,24]{1,2,0:T(8,128)} %param.4) | copy-start | bytes 147460
  23.6 26.4 %collective-permute-start.6 = (f32[10,32,128]{2,1,0:T(8,128)}, f32[10,32,128]{2,1,0:T(8,128)}, u32[]{:S(2)}, u32[]{:S(2)}) collective-permute-start(f32[10,32,128]{2,1,0:T(8,128)} %get-tuple-element.37), channel_id=1, source_target_pairs={{0,4},{4,8},{8,12},{12,16},{16,20},{20,24},{24,28},{1,5},{5,9},{9,... | collective-permute-start | bytes 491528 | tf_op jit(solution)/shard_map/ppermute | solution.py:31
  31.2 0.7 copy-start.5
  33.5 2.5 slice-start.2
  33.5 37.8 %slice-start = ((s8[7077888]{0:T(1024)(128)(4,1)}), s8[2883584]{0:T(1024)(128)(4,1)S(1)}, s32[]{:S(2)}) async-start(s8[7077888]{0:T(1024)(128)(4,1)} %bitcast.17), calls=%async_computation.2 | async-start | bytes 5767168
  50.0 8.4 %collective-permute-start.7 = (f32[10,32,128]{2,1,0:T(8,128)}, f32[10,32,128]{2,1,0:T(8,128)S(1)}, u32[]{:S(2)}, u32[]{:S(2)}) collective-permute-start(f32[10,32,128]{2,1,0:T(8,128)} %get-tuple-element.36), channel_id=1, source_target_pairs={{4,0},{8,4},{12,8},{16,12},{20,16},{24,20},{28,24},{5,1},{9,5},{13... | collective-permute-start | bytes 491528 | tf_op jit(solution)/shard_map/ppermute | solution.py:31
  58.4 5.1 %copy-start.4 = (f32[68,32,128]{2,1,0:T(8,128)}, f32[68,32,128]{2,1,0:T(8,128)S(1)}, u32[]{:S(2)}) copy-start(f32[68,32,128]{2,1,0:T(8,128)S(1)} %constant_dynamic-update-slice_fusion.phi_own) | copy-start | bytes 3342340
  58.4 13.0 %slice-start.1 = ((s8[7077888]{0:T(1024)(128)(4,1)}), s8[4194304]{0:T(1024)(128)(4,1)S(1)}, s32[]{:S(2)}) async-start(s8[7077888]{0:T(1024)(128)(4,1)} %bitcast.17), calls=%async_computation.3 | async-start | bytes 8388608
  58.6 47.1 %collective-permute-start.8 = (f32[68,10,128]{2,0,1:T(8,128)S(1)}, f32[68,10,128]{2,0,1:T(8,128)S(1)}, u32[]{:S(2)}, u32[]{:S(2)}) collective-permute-start(f32[68,10,128]{2,0,1:T(8,128)S(1)} %copy.45), channel_id=1, source_target_pairs={{0,1},{1,2},{2,3},{4,5},{5,6},{6,7},{8,9},{9,10},{10,11},{12,13},{... | collective-permute-start | bytes 1044488 | tf_op jit(solution)/shard_map/ppermute | solution.py:31
  65.1 38.8 %collective-permute-start.5 = (f32[3,3,2,8,384]{4,3,2,1,0:T(8,128)S(1)}, f32[3,3,2,8,384]{4,3,2,1,0:T(8,128)S(1)}, u32[]{:S(2)}, u32[]{:S(2)}) collective-permute-start(f32[3,3,2,8,384]{4,3,2,1,0:T(8,128)S(1)} %slice.144), channel_id=1, source_target_pairs={{4,0},{8,4},{12,8},{16,12},{20,16},{24,20},{28,24},{5,1},{9,5},{13... | collective-permute-start | bytes 663560 | tf_op jit(solution)/shard_map/ppermute | solution.py:31
  66.4 35.4 %collective-permute-start.4 = (f32[3,3,1,8,384]{4,3,2,1,0:T(8,128)S(1)}, f32[3,3,1,8,384]{4,3,2,1,0:T(8,128)S(1)}, u32[]{:S(2)}, u32[]{:S(2)}) collective-permute-start(f32[3,3,1,8,384]{4,3,2,1,0:T(8,128)S(1)} %slice.141), channel_id=1, source_target_pairs={{0,4},{4,8},{8,12},{12,16},{16,20},{20,24},{24,28},{1,5},{5,9},{9,... | collective-permute-start | bytes 331784 | tf_op jit(solution)/shard_map/ppermute | solution.py:31
  71.4 32.6 %copy-start.3 = (f32[3,3,3,32,384]{4,3,2,1,0:T(8,128)S(1)}, f32[3,3,3,32,384]{4,3,2,1,0:T(8,128)}, u32[]{:S(2)}) copy-start(f32[3,3,3,32,384]{4,3,2,1,0:T(8,128)} %get-tuple-element.21) | copy-start | bytes 3981316
  101.8 3.9 %copy-start = (f32[32,384]{1,0:T(8,128)}, f32[32,384]{1,0:T(8,128)S(1)}, u32[]{:S(2)}) copy-start(f32[32,384]{1,0:T(8,128)S(1)} %get-tuple-element.11) | copy-start | bytes 147460
  101.8 2.2 copy-start.2
  101.8 9.1 %collective-permute-start.9 = (f32[68,10,128]{2,0,1:T(8,128)S(1)}, f32[68,10,128]{2,0,1:T(8,128)}, u32[]{:S(2)}, u32[]{:S(2)}) collective-permute-start(f32[68,10,128]{2,0,1:T(8,128)S(1)} %copy.46), channel_id=1, source_target_pairs={{1,0},{2,1},{3,2},{5,4},{6,5},{7,6},{9,8},{10,9},{11,10},{13,12},{... | collective-permute-start | bytes 1044488 | tf_op jit(solution)/shard_map/ppermute | solution.py:31
  105.7 18.2 %copy-start.6 = (f32[68,10,128]{2,0,1:T(8,128)}, f32[68,10,128]{2,0,1:T(8,128)S(1)}, u32[]{:S(2)}) copy-start(f32[68,10,128]{2,0,1:T(8,128)S(1)} %collective-permute-done.8) | copy-start | bytes 1044484
  173.4 7.2 %copy-start.1 = (f32[32,384]{1,0:T(8,128)S(1)}, f32[32,384]{1,0:T(8,128)}, u32[]{:S(2)}) copy-start(f32[32,384]{1,0:T(8,128)} %copy-done) | copy-start | bytes 147460
  174.5 20.6 %collective-permute-start.10 = (f32[68,10,128]{2,0,1:T(8,128)}, f32[68,10,128]{2,0,1:T(8,128)S(1)}, u32[]{:S(2)}, u32[]{:S(2)}) collective-permute-start(f32[68,10,128]{2,0,1:T(8,128)} %copy.52), channel_id=1, source_target_pairs={{0,1},{1,2},{2,3},{4,5},{5,6},{6,7},{8,9},{9,10},{10,11},{12,13},{... | collective-permute-start | bytes 1044488 | tf_op jit(solution)/shard_map/ppermute | solution.py:31
  178.7 17.3 %collective-permute-start.11 = (f32[68,10,128]{2,0,1:T(8,128)}, f32[68,10,128]{2,0,1:T(8,128)S(1)}, u32[]{:S(2)}, u32[]{:S(2)}) collective-permute-start(f32[68,10,128]{2,0,1:T(8,128)} %copy.53), channel_id=1, source_target_pairs={{1,0},{2,1},{3,2},{5,4},{6,5},{7,6},{9,8},{10,9},{11,10},{13,12},{... | collective-permute-start | bytes 1044488 | tf_op jit(solution)/shard_map/ppermute | solution.py:31
  182.5 10.2 %all-to-all-start = ((f32[32,1,128]{2,1,0:T(1,128)}), f32[32,1,128]{2,1,0:T(1,128)S(1)}, u32[]{:S(2)}, u32[]{:S(2)}) async-start(f32[32,1,128]{2,1,0:T(1,128)} %broadcast_in_dim.17), calls=%async_computation | async-start | bytes 32768 | tf_op jit(solution)/shard_map/all_to_all | solution.py:366
